TPU v7x, 1024 devices: a whole 4x8x16 slice. The times are simulated.
1024 devices in a mesh: slab: 64 (over y_lo, z, core), energy: 16 (over x, y_hi).
Axes of the slice: x: 4, y: 8 (y_hi: 4, y_lo: 2; y = y_hi * 2 + y_lo), z: 16, core: 2. Of those that a mesh axis runs over, the one named last changes fastest.
Arguments:
- energy: float32 [64], P('energy'), may hold values from -0.1 to 0.1
- onsite: float32 [8192, 128], P('slab'), may hold values from -1.2 to 0.08, as said below
- coupling: bfloat16 [8192, 128], P('slab'), may hold values from -0.140625 to 0.140625
- atom_of: int32 [8192], P('slab'), may hold values from 0 to 31
- strength: float32 [2048], P('slab'), may hold values from 0.5 to 1.5
- previous: bfloat16 [64, 2, 8192, 128], P('energy', None, 'slab'), may hold values from -0.29882812 to 0.29882812
- phonon_weight: float32 [4], replicated, may hold values from 0.01 to 0.05
- offsets: int32 [4], replicated, may hold values from 1 to 4, as said below
- in_flight: bfloat16 [32, 2, 8192, 128], P('energy', None, 'slab'), may hold values from -0.3 to 1.4, as said below
Outputs:
- green_last: bfloat16 [32, 2, 8192, 128], P('energy', None, 'slab')
- diagonal: float32 [64, 2, 8192], P('energy', None, 'slab')
Inputs may be any that keep to these rules, and one draw needn't show every extreme that they name: The largest of the 4 offsets equals 4 in every draw. `onsite`: each 128 x 128 block is symmetric and its diagonal lies in -1.2 to -0.8. `in_flight`: in each 128 x 128 block the diagonal's real part lies in 0.7 to 1.4 and its imaginary part in -0.3 to -0.05.
All inputs are finite; a program needn't handle non-finite values.
Results may differ from a plain program's by a relative error of at most 0.0028.
The roundings to bfloat16 on the way count: a program that leaves them out, or rounds other values in their place, can miss the bound.
Values may be sent and summed in bfloat16 or wider, within the bound.
No kernel may reach another device: no remote copies, remote signals or barrier semaphores. Data moves between devices by JAX's collectives and lax.ppermute only.
A program may use at most 32 MiB of HBM per device.

v0:
```python
import jax
import jax.numpy as jnp
from jax import lax
from jax.sharding import PartitionSpec as P

B = 128
ATOMS = 32
EB = 2
TICKS = 2
MODES = 4
OMAX = 4
E_DEV = 4


broadening = 0.05


def with_halo(array, sides, width):
    for axis, dim in sides:
        devices, length = (lax.axis_size(axis), array.shape[dim])
        up = [(i, (i + 1) % devices) for i in range(devices - 1)]
        down = [(j, i) for i, j in up]
        last = lax.slice_in_dim(array, length - width, length, axis=dim)
        first = lax.slice_in_dim(array, 0, width, axis=dim)
        before = lax.ppermute(last, axis, up)
        after = lax.ppermute(first, axis, down)
        array = jnp.concatenate([before, array, after], axis=dim)
    return array


def from_behind(block, axis, distance):
    devices = range(lax.axis_size(axis))
    route = [(i - distance, i) for i in devices if i - distance in devices]
    return lax.ppermute(block, axis, route)


def half_product(left_side, right_side):
    return jnp.matmul(left_side, right_side, preferred_element_type=jnp.float32)


def complex_product(left_side, right_side):
    left_real = left_side[..., 0, :, :]
    left_imag = left_side[..., 1, :, :]
    right_real = right_side[..., 0, :, :]
    right_imag = right_side[..., 1, :, :]
    real_part = half_product(left_real, right_real) - half_product(left_imag, right_imag)
    imag_part = half_product(left_real, right_imag) + half_product(left_imag, right_real)
    return jnp.stack([real_part, imag_part], axis=-3)


def advance(incoming, coupling, onsite, self_energy, energies):
    identity = jnp.eye(B, dtype=jnp.float32)
    mixed_block = half_product(coupling, incoming).astype(jnp.bfloat16)
    coupled = jnp.einsum("ecij,kj->ecik", mixed_block, coupling, preferred_element_type=jnp.float32)
    shifted = energies[..., None, None] * identity - onsite
    real_part = shifted - self_energy[..., 0, :, :] - coupled[..., 0, :, :]
    imag_part = broadening * identity - self_energy[..., 1, :, :] - coupled[..., 1, :, :]
    level_gap = energies[..., None] - jnp.diagonal(onsite, axis1=-2, axis2=-1)
    denominator = level_gap * level_gap + broadening * broadening
    start_real = level_gap / denominator
    start_imag = -broadening / denominator
    scaled_real = real_part * start_real[..., None, :] - imag_part * start_imag[..., None, :]
    scaled_imag = real_part * start_imag[..., None, :] + imag_part * start_real[..., None, :]
    rest_real = 2.0 * identity - scaled_real
    rest_imag = -scaled_imag
    first_real = start_real[..., :, None] * rest_real - start_imag[..., :, None] * rest_imag
    first_imag = start_real[..., :, None] * rest_imag + start_imag[..., :, None] * rest_real
    system = jnp.stack([real_part, imag_part], axis=-3).astype(jnp.bfloat16)
    first_guess = jnp.stack([first_real, first_imag], axis=-3).astype(jnp.bfloat16)
    product = complex_product(system, first_guess)
    residue = jnp.stack(
        [2.0 * identity - product[..., 0, :, :], -product[..., 1, :, :]], axis=-3
    ).astype(jnp.bfloat16)
    return complex_product(first_guess, residue).astype(jnp.bfloat16)


def body(energy, onsite, coupling, atom_of, strength, previous, phonon_weight, offsets, in_flight):
    slab_index = lax.axis_index("slab")
    matches = (atom_of[:, None] == jnp.arange(ATOMS, dtype=jnp.int32)[None, :]).astype(jnp.float32)
    orbital_scale = jnp.dot(matches, strength, precision=lax.Precision.HIGHEST)
    pair_scale = orbital_scale[:, None] * orbital_scale[None, :]
    widened = with_halo(previous, (("energy", 0),), OMAX)
    phonon = jnp.zeros((E_DEV, 2, B, B), jnp.float32)
    for member in range(MODES):
        lower_part = lax.dynamic_slice_in_dim(widened, OMAX - offsets[member], E_DEV, 0).astype(
            jnp.float32
        )
        upper_part = lax.dynamic_slice_in_dim(widened, OMAX + offsets[member], E_DEV, 0).astype(
            jnp.float32
        )
        phonon = phonon + phonon_weight[member] * (lower_part + upper_part)
    self_energy = phonon * pair_scale
    diagonals = jnp.zeros((E_DEV, 2, B), jnp.float32)
    green_block = in_flight
    for tick_index in range(TICKS):
        batch_index = jnp.mod(tick_index - slab_index, TICKS)
        first_energy = batch_index * EB
        self_batch = lax.dynamic_slice_in_dim(self_energy, first_energy, EB, 0)
        energy_batch = lax.dynamic_slice_in_dim(energy, first_energy, EB, 0)
        if tick_index == 0:
            arriving = in_flight
        else:
            arriving = from_behind(green_block, "slab", 1)
        green_block = advance(arriving, coupling, onsite, self_batch, energy_batch)
        green_diagonal = jnp.diagonal(green_block, axis1=-2, axis2=-1).astype(jnp.float32)
        diagonals = lax.dynamic_update_slice_in_dim(diagonals, green_diagonal, first_energy, 0)
    return (green_block, diagonals)


def solution(mesh):
    placed = (
        P("energy"),
        P("slab", None),
        P("slab", None),
        P("slab"),
        P("slab"),
        P("energy", None, "slab", None),
        P(),
        P(),
        P("energy", None, "slab", None),
    )
    return jax.shard_map(
        body,
        mesh=mesh,
        in_specs=placed,
        out_specs=(P("energy", None, "slab", None), P("energy", None, "slab")),
        check_vma=False,
    )
```

profile of v0, /device:TPU:16, one launch (start us, length us, event | category | flops | bytes accessed | tf_op | source)
XLA Modules:
  0.0 73.4 jit_solution(13924218021204490048)
XLA Ops:
  0.6 5.8 %collective-permute-start = (bf16[4,2,128,128]{3,2,1,0:T(8,128)(2,1)}, bf16[4,2,128,128]{3,2,1,0:T(8,128)(2,1)S(1)}, u32[]{:S(2)}, u32[]{:S(2)}) collective-permute-start(bf16[4,2,128,128]{3,2,1,0:T(8,128)(2,1)} %param.14), channel_id=1, source_target_pairs={{0,1},{1,2},{2,3},{3,4},{4,5},{5,6},{6,7},{7,8},{8,9},{9,10},{10,1... | collective-permute-start | bytes 786440 | tf_op jit(solution)/shard_map/ppermute | solution.py:25
  6.5 10.5 %collective-permute-start.1 = (bf16[4,2,128,128]{3,2,1,0:T(8,128)(2,1)}, bf16[4,2,128,128]{3,2,1,0:T(8,128)(2,1)S(1)}, u32[]{:S(2)}, u32[]{:S(2)}) collective-permute-start(bf16[4,2,128,128]{3,2,1,0:T(8,128)(2,1)} %param.14), channel_id=1, source_target_pairs={{1,0},{2,1},{3,2},{4,3},{5,4},{6,5},{7,6},{8,7},{9,8},{10,9},{11,1... | collective-permute-start | bytes 786440 | tf_op jit(solution)/shard_map/ppermute | solution.py:26
  17.1 0.9 %convolution_bitcast_fusion = f32[128]{0:T(128)S(1)} fusion(s32[128]{0:T(128)} %param.12, f32[32]{0:T(128)} %param.13), kind=kOutput, calls=%fused_computation.33 | convolution fusion | flops 53248 | bytes 1152 | tf_op jit(solution)/shard_map/dot_general | solution.py:80
  18.1 1.9 %gather_fusion = f32[128]{0:T(128)S(1)} fusion(f32[128,128]{1,0:T(8,128)} %param.10, s32[128]{0:T(128)S(1)} %or_bitcast_fusion), kind=kCustom, calls=%fused_computation | custom fusion | bytes 2048 | tf_op jit(solution)/shard_map/jit(diagonal)/cond/branch_0_fun/gather | solution.py:58
  20.0 1.1 %fusion.1 = f32[2,2,128,128]{3,2,1,0:T(8,128)S(1)} fusion(bf16[2,2,128,128]{3,2,1,0:T(8,128)(2,1)S(1)} %copy-done, bf16[128,128]{1,0:T(8,128)(2,1)} %param.11), kind=kOutput, calls=%fused_computation.6 | convolution fusion | flops 33619968 | bytes 425984 | tf_op jit(solution)/shard_map/ecij,kj->ecik/dot_general | solution.py:54
  21.2 0.8 %fusion.61 = (f32[2]{0:T(128)S(1)}, f32[2]{0:T(128)S(1)}) fusion(f32[4]{0:T(128)} %param.9, s32[]{:T(128)S(6)} %select_n.68, s32[]{:T(128)S(6)} %select_n.58), kind=kLoop, calls=%fused_computation.106 | loop fusion | bytes 40 | tf_op jit(solution)/shard_map/dynamic_slice | solution.py:99
  22.1 1.4 %fusion.60 = (s32[1]{0:T(128)}, s32[1]{0:T(128)}, s32[1]{0:T(128)}, s32[1]{0:T(128)}) fusion(s32[4]{0:T(128)} %param.16), kind=kLoop, calls=%fused_computation.105 | loop fusion | bytes 32 | tf_op jit(solution)/shard_map/slice | solution.py:85
  23.5 1.5 %fusion.59 = (f32[1]{0:T(128)}, f32[1]{0:T(128)}, f32[1]{0:T(128)}, f32[1]{0:T(128)}) fusion(f32[4]{0:T(128)} %param.15), kind=kLoop, calls=%fused_computation.104 | loop fusion | bytes 32 | tf_op jit(solution)/shard_map/slice | solution.py:91
  34.9 1.0 %constant_dynamic-update-slice_fusion.1 = bf16[12,2,128,128]{3,2,1,0:T(8,128)(2,1)S(1)} fusion(bf16[12,2,128,128]{3,2,1,0:T(8,128)(2,1)S(1)} %constant_dynamic-update-slice_fusion.2, bf16[4,2,128,128]{3,2,1,0:T(8,128)(2,1)} %param.14), kind=kLoop, calls=%fused_computation.90 | loop fusion | bytes 524288
  36.0 2.8 %add_multiply_fusion = f32[4,2,128,128]{3,2,1,0:T(8,128)S(1)} fusion(f32[128,128]{1,0:T(8,128)S(1)} %broadcast_multiply_fusion, bf16[12,2,128,128]{3,2,1,0:T(8,128)(2,1)S(1)} %constant_dynamic-update-slice_fusion, s32[]{:T(128)S(6)} %select_n.66, s32[]{:T(128)S(6)} %select_n.65, f32[]{:T(128)} %bitcast.16, s32[]{:T(128)S(6)} %select_n.64, s32[]{:T(128)S(6)} %select_n.63, ...), kind=kLoop, calls=%fused_computation.34 | loop fusion | flops 2621440 | bytes 2687024 | tf_op jit(solution)/shard_map/mul | solution.py:92
  38.8 1.0 %fusion.23 = (bf16[2,128,128]{2,1,0:T(8,128)(2,1)S(1)}, f32[2,1,128,128]{3,2,1,0:T(8,128)S(1)}, f32[2,1,128,128]{3,2,1,0:T(8,128)S(1)}) fusion(f32[2,128]{1,0:T(2,128)S(1)} %get-tuple-element.13, f32[2,128]{1,0:T(2,128)S(1)} %get-tuple-element.12, f32[128,128]{1,0:T(8,128)S(1)} %fusion.40, f32[2,2,128,128]{3,2,1,0:T(8,128)S(1)} %fusion.1, ...), kind=kLoop, calls=%fused_computation.57 | loop fusion | flops 589824 | bytes 1118728 | tf_op jit(solution)/shard_map/squeeze | solution.py:45
  40.3 0.2 fusion.9
  40.9 0.2 fusion.19
  41.3 1.3 %collective-permute-start.2 = (bf16[2,2,128,128]{3,2,0,1:T(8,128)(2,1)S(1)}, bf16[2,2,128,128]{3,2,0,1:T(8,128)(2,1)S(1)}, u32[]{:S(2)}, u32[]{:S(2)}) collective-permute-start(bf16[2,2,128,128]{3,2,0,1:T(8,128)(2,1)S(1)} %pad_maximum_fusion), channel_id=1, source_target_pairs={{0,16},{16,32},{32,48},{48,64},{64,80},{80,96},{96,112},{112,128},... | collective-permute-start | bytes 393224 | tf_op jit(solution)/shard_map/ppermute | solution.py:34
  42.6 9.4 %copy.12 = bf16[2,2,128,128]{1,0,3,2:T(2,128)(2,1)} copy(bf16[2,2,128,128]{3,2,0,1:T(8,128)(2,1)S(1)} %pad_maximum_fusion) | data formatting | bytes 262144 | tf_op jit(solution)/shard_map/stack | solution.py:48
  52.0 4.3 %gather_fusion.1 = bf16[128,2,2]{2,1,0:T(2,128)(2,1)S(1)} fusion(bf16[2,2,128,128]{1,0,3,2:T(2,128)(2,1)} %copy.12, s32[128]{0:T(128)S(1)} %or_bitcast_fusion), kind=kCustom, calls=%fused_computation.1 | custom fusion | bytes 3072 | tf_op jit(solution)/shard_map/jit(diagonal)/gather | solution.py:105
  56.4 0.3 fusion.3
  57.3 0.2 fusion.8
  57.7 0.2 fusion.13
  58.0 0.2 fusion.17
  58.3 9.4 %copy.14 = bf16[2,2,128,128]{1,0,3,2:T(2,128)(2,1)} copy(bf16[2,2,128,128]{3,2,0,1:T(8,128)(2,1)S(1)} %pad_maximum_fusion.1) | data formatting | bytes 262144 | tf_op jit(solution)/shard_map/stack | solution.py:48
  67.8 0.7 copy.16
  68.4 4.3 %gather_fusion.2 = bf16[128,2,2]{2,1,0:T(2,128)(2,1)S(1)} fusion(bf16[2,2,128,128]{1,0,3,2:T(2,128)(2,1)} %copy.14, s32[128]{0:T(128)S(1)} %or_bitcast_fusion), kind=kCustom, calls=%fused_computation.2 | custom fusion | bytes 3072 | tf_op jit(solution)/shard_map/jit(diagonal)/gather | solution.py:105
  72.8 0.6 copy-done.3
  (41 shorter events, 2.8 us)
Async XLA Ops:
  0.6 19.4 %copy-start = (bf16[2,2,128,128]{3,2,1,0:T(8,128)(2,1)S(1)}, bf16[2,2,128,128]{3,2,1,0:T(8,128)(2,1)}, u32[]{:S(2)}) copy-start(bf16[2,2,128,128]{3,2,1,0:T(8,128)(2,1)} %param.17) | copy-start | bytes 393220
  0.6 34.2 %collective-permute-start = (bf16[4,2,128,128]{3,2,1,0:T(8,128)(2,1)}, bf16[4,2,128,128]{3,2,1,0:T(8,128)(2,1)S(1)}, u32[]{:S(2)}, u32[]{:S(2)}) collective-permute-start(bf16[4,2,128,128]{3,2,1,0:T(8,128)(2,1)} %param.14), channel_id=1, source_target_pairs={{0,1},{1,2},{2,3},{3,4},{4,5},{5,6},{6,7},{7,8},{8,9},{9,10},{10,1... | collective-permute-start | bytes 786440 | tf_op jit(solution)/shard_map/ppermute | solution.py:25
  6.5 29.4 %collective-permute-start.1 = (bf16[4,2,128,128]{3,2,1,0:T(8,128)(2,1)}, bf16[4,2,128,128]{3,2,1,0:T(8,128)(2,1)S(1)}, u32[]{:S(2)}, u32[]{:S(2)}) collective-permute-start(bf16[4,2,128,128]{3,2,1,0:T(8,128)(2,1)} %param.14), channel_id=1, source_target_pairs={{1,0},{2,1},{3,2},{4,3},{5,4},{6,5},{7,6},{8,7},{9,8},{10,9},{11,1... | collective-permute-start | bytes 786440 | tf_op jit(solution)/shard_map/ppermute | solution.py:26
  35.9 20.5 %copy-start.2 = (bf16[128,128]{1,0:T(8,128)(2,1)S(1)}, bf16[128,128]{1,0:T(8,128)(2,1)}, u32[]{:S(2)}) copy-start(bf16[128,128]{1,0:T(8,128)(2,1)} %param.11) | copy-start | bytes 98308
  36.0 20.8 %copy-start.1 = (f32[128,128]{1,0:T(8,128)S(1)}, f32[128,128]{1,0:T(8,128)}, u32[]{:S(2)}) copy-start(f32[128,128]{1,0:T(8,128)} %param.10) | copy-start | bytes 196612
  41.3 15.2 %collective-permute-start.2 = (bf16[2,2,128,128]{3,2,0,1:T(8,128)(2,1)S(1)}, bf16[2,2,128,128]{3,2,0,1:T(8,128)(2,1)S(1)}, u32[]{:S(2)}, u32[]{:S(2)}) collective-permute-start(bf16[2,2,128,128]{3,2,0,1:T(8,128)(2,1)S(1)} %pad_maximum_fusion), channel_id=1, source_target_pairs={{0,16},{16,32},{32,48},{48,64},{64,80},{80,96},{96,112},{112,128},... | collective-permute-start | bytes 393224 | tf_op jit(solution)/shard_map/ppermute | solution.py:34
  72.8 0.6 copy-start.3
where the time goes:
time: 74.1 us; the launch traced here: 73.4 us
  local copies, waits for them, and re-layouts  35.5 us (48%)
  starting transfers between devices  17.6 us (24%)
  between operations  10.8 us (15%)
  matrix products  4.83 us (7%)
  other arithmetic  4.64 us (6%)
    another operation x2, local copies, waits for them, and re-layouts, complex_product(): return jnp.stack([real_part, imag_part], axis=-3)  18.9 us
    ppermute x1, starting transfers between devices, with_halo(): after = lax.ppermute(first, axis, down)  10.5 us
    gather x2, local copies, waits for them, and re-layouts, body(): jnp.diagonal(green_block, axis1=-2, axis2=-1).astype(jnp.float32)  8.51 us
    ppermute x1, starting transfers between devices, with_halo(): before = lax.ppermute(last, axis, up)  5.84 us
    mul x1, other arithmetic, body(): self_energy = phonon * pair_scale  2.84 us
    dot_general x16, matrix products, half_product(): return jnp.matmul(left_side, right_side, preferred_element_type=jnp.float32)  2.52 us
    unnamed x11, local copies, waits for them, and re-layouts  2.3 us
    gather x1, local copies, waits for them, and re-layouts, advance(): level_gap = energies[..., None] - jnp.diagonal(onsite, axis1=-2, axis2=-1)  1.94 us
  transfers between devices with their start and end apart: 3, of which 0 were waited for; matrix products, arithmetic and copies ran while one was open for 31% of the time, Pallas kernels for 0%

commit v1 on v0

v1 whole, which is shorter than its diff:
```python
import jax
import jax.numpy as jnp
from jax import lax
from jax.experimental import pallas as pl
from jax.experimental.pallas import tpu as pltpu
from jax.sharding import PartitionSpec as P

B = 128
ATOMS = 32
EB = 2
MODES = 4
OMAX = 4
E_DEV = 4
CHUNK = 32

broadening = 0.05
f32 = jnp.float32
bf16 = jnp.bfloat16

VMEM = pltpu.MemorySpace.VMEM
SMEM = pltpu.MemorySpace.SMEM


def offset_weights(weight_ref, offset_ref):
    sums = {}
    for distance in range(1, OMAX + 1):
        total = jnp.float32(0.0)
        for mode in range(MODES):
            total = total + jnp.where(offset_ref[mode] == distance, weight_ref[mode], 0.0)
        sums[distance] = total
    return sums


def weighted(terms):
    total = None
    for factor, value in terms:
        part = factor * value
        total = part if total is None else total + part
    return total


def partial_kernel(slab_ref, weight_ref, offset_ref, previous_ref, up0_ref, down0_ref, up1_ref, down1_ref):
    sums = offset_weights(weight_ref, offset_ref)

    def fill(ups, downs):
        for part in range(2):
            for row in range(0, B, CHUNK):
                rows = pl.ds(row, CHUNK)
                values = [previous_ref[e, part, rows, :].astype(f32) for e in range(E_DEV)]
                for target in range(E_DEV):
                    up = weighted([(sums[OMAX + target - e], values[e]) for e in range(target, E_DEV)])
                    down = weighted([(sums[e + OMAX - target], values[e]) for e in range(0, target + 1)])
                    ups[target // EB][target % EB, part, rows, :] = up.astype(bf16)
                    downs[target // EB][target % EB, part, rows, :] = down.astype(bf16)

    parity = slab_ref[0]

    @pl.when(parity == 0)
    def _():
        fill((up0_ref, up1_ref), (down0_ref, down1_ref))

    @pl.when(parity != 0)
    def _():
        fill((up1_ref, up0_ref), (down1_ref, down0_ref))


def mixed_coupling(coupling, blocks):
    wide = jnp.concatenate(blocks, axis=1)
    mixed = jnp.dot(coupling, wide, preferred_element_type=f32).astype(bf16)
    tall = jnp.concatenate([mixed[:, i * B : (i + 1) * B] for i in range(len(blocks))], axis=0)
    both = lax.dot_general(tall, coupling, (((1,), (1,)), ((), ())), preferred_element_type=f32)
    return [both[i * B : (i + 1) * B, :] for i in range(len(blocks))]


def diagonal_mask():
    return lax.broadcasted_iota(jnp.int32, (B, B), 0) == lax.broadcasted_iota(jnp.int32, (B, B), 1)


def local_kernel(
    slab_ref, weight_ref, offset_ref, energy_ref, onsite_ref, coupling_ref, atom_ref, strength_ref,
    previous_ref, flight_ref, base_ref, product_ref, twice_ref, pair_ref,
):
    sums = offset_weights(weight_ref, offset_ref)
    on_diagonal = diagonal_mask()
    atoms = lax.broadcasted_iota(jnp.int32, (ATOMS, ATOMS), 0) == lax.broadcasted_iota(jnp.int32, (ATOMS, ATOMS), 1)
    strength_column = jnp.sum(jnp.where(atoms, strength_ref[...], 0.0), axis=1, keepdims=True)
    matches = lax.broadcasted_iota(jnp.int32, (ATOMS, B), 0) == atom_ref[...]
    scale_row = jnp.sum(jnp.where(matches, strength_column, 0.0), axis=0, keepdims=True)
    scale_column = jnp.sum(jnp.where(on_diagonal, scale_row, 0.0), axis=1, keepdims=True)
    pair_ref[...] = scale_column * scale_row

    level_row = jnp.sum(jnp.where(on_diagonal, onsite_ref[...], 0.0), axis=0, keepdims=True)
    level_column = jnp.sum(jnp.where(on_diagonal, onsite_ref[...], 0.0), axis=1, keepdims=True)

    def start(gap):
        denominator = gap * gap + broadening * broadening
        return gap / denominator, -broadening / denominator

    for e in range(E_DEV):
        row_real, row_imag = start(energy_ref[e] - level_row)
        column_real, column_imag = start(energy_ref[e] - level_column)
        product_ref[e, 0] = column_real * row_real - column_imag * row_imag
        product_ref[e, 1] = column_real * row_imag + column_imag * row_real
        twice_ref[e, 0:1, :] = 2.0 * row_real
        twice_ref[e, 1:2, :] = 2.0 * row_imag

    for row in range(0, B, CHUNK):
        rows = pl.ds(row, CHUNK)
        pair = pair_ref[rows, :]
        mask = (lax.broadcasted_iota(jnp.int32, (CHUNK, B), 0) + row) == lax.broadcasted_iota(jnp.int32, (CHUNK, B), 1)
        onsite = onsite_ref[rows, :]
        for part in range(2):
            values = [previous_ref[e, part, rows, :].astype(f32) for e in range(E_DEV)]
            for target in range(E_DEV):
                phonon = weighted([(sums[abs(target - e)], values[e]) for e in range(E_DEV) if e != target])
                if part == 0:
                    head = jnp.where(mask, energy_ref[target], 0.0) - onsite
                else:
                    head = jnp.where(mask, jnp.float32(broadening), 0.0)
                base_ref[target, part, rows, :] = head - phonon * pair

    first = slab_ref[0] * EB
    coupled = mixed_coupling(coupling_ref[...], [flight_ref[m, c] for m in range(EB) for c in range(2)])
    for m in range(EB):
        for c in range(2):
            base_ref[first + m, c] = base_ref[first + m, c] - coupled[m * 2 + c]


def complex_rows(real, imag):
    return jnp.concatenate([real, imag], axis=1)


def complex_square(real, imag):
    top = jnp.concatenate([real, imag], axis=1)
    bottom = jnp.concatenate([-imag, real], axis=1)
    return jnp.concatenate([top, bottom], axis=0)


def green_of(real, imag, product_real, product_imag, twice_real, twice_imag, on_diagonal):
    first_real = jnp.where(on_diagonal, twice_real, 0.0) - (real * product_real - imag * product_imag)
    first_imag = jnp.where(on_diagonal, twice_imag, 0.0) - (real * product_imag + imag * product_real)
    first_real = first_real.astype(bf16)
    first_imag = first_imag.astype(bf16)
    product = jnp.dot(
        complex_rows(real.astype(bf16), imag.astype(bf16)), complex_square(first_real, first_imag),
        preferred_element_type=f32,
    )
    residue_real = (jnp.where(on_diagonal, 2.0, 0.0) - product[:, :B]).astype(bf16)
    residue_imag = (-product[:, B:]).astype(bf16)
    green = jnp.dot(
        complex_rows(first_real, first_imag), complex_square(residue_real, residue_imag),
        preferred_element_type=f32,
    ).astype(bf16)
    return green[:, :B], green[:, B:]


def green_diagonal(green, on_diagonal):
    return jnp.sum(jnp.where(on_diagonal, green.astype(f32), 0.0), axis=0, keepdims=True)


def first_tick_kernel(slab_ref, base_ref, product_ref, twice_ref, pair_ref, low_ref, high_ref, green_ref, diagonal_ref):
    first = slab_ref[0] * EB
    on_diagonal = diagonal_mask()
    pair = pair_ref[...]
    for m in range(EB):
        e = first + m
        system = [
            base_ref[e, c] - (low_ref[m, c].astype(f32) + high_ref[m, c].astype(f32)) * pair for c in range(2)
        ]
        greens = green_of(
            system[0], system[1], product_ref[e, 0], product_ref[e, 1],
            twice_ref[e, 0:1, :], twice_ref[e, 1:2, :], on_diagonal,
        )
        for c in range(2):
            green_ref[m, c] = greens[c]
            diagonal_ref[m, c : c + 1, :] = green_diagonal(greens[c], on_diagonal)


def last_tick_kernel(
    slab_ref, base_ref, product_ref, twice_ref, pair_ref, low_ref, high_ref, arriving_ref, coupling_ref,
    earlier_ref, green_ref, diagonal_ref,
):
    earlier = slab_ref[0] * EB
    first = (1 - slab_ref[0]) * EB
    on_diagonal = diagonal_mask()
    pair = pair_ref[...]
    coupled = mixed_coupling(coupling_ref[...], [arriving_ref[m, c] for m in range(EB) for c in range(2)])
    for m in range(EB):
        e = first + m
        system = [
            base_ref[e, c]
            - (low_ref[m, c].astype(f32) + high_ref[m, c].astype(f32)) * pair
            - coupled[m * 2 + c]
            for c in range(2)
        ]
        greens = green_of(
            system[0], system[1], product_ref[e, 0], product_ref[e, 1],
            twice_ref[e, 0:1, :], twice_ref[e, 1:2, :], on_diagonal,
        )
        diagonal_ref[earlier + m] = earlier_ref[m]
        for c in range(2):
            green_ref[m, c] = greens[c]
            diagonal_ref[e, c : c + 1, :] = green_diagonal(greens[c], on_diagonal)


def spec(space):
    return pl.BlockSpec(memory_space=space)


def call(kernel, scalars, arrays, outs, name):
    return pl.pallas_call(
        kernel,
        in_specs=[spec(SMEM)] * len(scalars) + [spec(VMEM)] * len(arrays),
        out_specs=[spec(VMEM)] * len(outs),
        out_shape=[jax.ShapeDtypeStruct(shape, dtype) for shape, dtype in outs],
        name=name,
    )(*scalars, *arrays)


def body(energy, onsite, coupling, atom_of, strength, previous, phonon_weight, offsets, in_flight):
    parity = (lax.axis_index("slab") & 1).astype(jnp.int32).reshape(1)
    devices = lax.axis_size("energy")
    up = [(i, i + 1) for i in range(devices - 1)]
    down = [(i + 1, i) for i in range(devices - 1)]
    slabs = lax.axis_size("slab")
    onward = [(i, i + 1) for i in range(slabs - 1)]
    half = (EB, 2, B, B)

    up0, down0, up1, down1 = call(
        partial_kernel, (parity, phonon_weight, offsets), (previous,), [(half, bf16)] * 4, "partials"
    )
    low0 = lax.ppermute(up0, "energy", up)
    high0 = lax.ppermute(down0, "energy", down)
    low1 = lax.ppermute(up1, "energy", up)
    high1 = lax.ppermute(down1, "energy", down)
    base, product, twice, pair = call(
        local_kernel,
        (parity, phonon_weight, offsets, energy),
        (onsite, coupling, atom_of.reshape(1, B), strength.reshape(1, ATOMS), previous, in_flight),
        [((E_DEV, 2, B, B), f32), ((E_DEV, 2, B, B), f32), ((E_DEV, 2, B), f32), ((B, B), f32)],
        "local",
    )
    green0, diagonal0 = call(
        first_tick_kernel, (parity,), (base, product, twice, pair, low0, high0),
        [(half, bf16), ((EB, 2, B), f32)], "first_tick",
    )
    arriving = lax.ppermute(green0, "slab", onward)
    green1, diagonals = call(
        last_tick_kernel, (parity,),
        (base, product, twice, pair, low1, high1, arriving, coupling, diagonal0),
        [(half, bf16), ((E_DEV, 2, B), f32)], "last_tick",
    )
    return green1, diagonals


def solution(mesh):
    placed = (
        P("energy"),
        P("slab", None),
        P("slab", None),
        P("slab"),
        P("slab"),
        P("energy", None, "slab", None),
        P(),
        P(),
        P("energy", None, "slab", None),
    )
    return jax.shard_map(
        body,
        mesh=mesh,
        in_specs=placed,
        out_specs=(P("energy", None, "slab", None), P("energy", None, "slab")),
        check_vma=False,
    )
```

time: 74.1 us -> 48.7 us (0.66)
  the two profiles are of different devices: /device:TPU:16 before, /device:TPU:14 now
where the time goes in v1:
time: 48.7 us; the launch traced here: 48.4 us
  starting transfers between devices  19.6 us (40%)
  waiting for transfers between devices  17.3 us (36%)
  Pallas kernels  9.42 us (19%)
  local copies, waits for them, and re-layouts  1.32 us (3%)
  between operations  0.74 us (2%)
    ppermute x1, waiting for transfers between devices, body(): arriving = lax.ppermute(green0, 'slab', onward)  17.3 us
    pallas_call x4, Pallas kernels, call(): pl.pallas_call(kernel, in_specs=[spec(SMEM)] * len(scalars) + [spec(VMEM)...  9.42 us
    ppermute x1, starting transfers between devices, body(): high1 = lax.ppermute(down1, 'energy', down)  6.46 us
    ppermute x1, starting transfers between devices, body(): low0 = lax.ppermute(up0, 'energy', up)  4.48 us
    ppermute x1, starting transfers between devices, body(): high0 = lax.ppermute(down0, 'energy', down)  4.35 us
    ppermute x1, starting transfers between devices, body(): low1 = lax.ppermute(up1, 'energy', up)  2.39 us
    ppermute x1, starting transfers between devices, body(): arriving = lax.ppermute(green0, 'slab', onward)  1.91 us
    unnamed x10, local copies, waits for them, and re-layouts  1.32 us
  transfers between devices with their start and end apart: 5, of which 1 were waited for; matrix products, arithmetic and copies ran while one was open for 0% of the time, Pallas kernels for 10%

profile of v1, /device:TPU:14, one launch (start us, length us, event | category | flops | bytes accessed | tf_op | source)
XLA Modules:
  0.0 48.4 jit_solution(7568961471988160797)
XLA Ops:
  0.6 1.9 %partials.1 = (bf16[2,2,128,128]{3,2,1,0:T(8,128)(2,1)}, bf16[2,2,128,128]{3,2,1,0:T(8,128)(2,1)}, bf16[2,2,128,128]{3,2,1,0:T(8,128)(2,1)}, bf16[2,2,128,128]{3,2,1,0:T(8,128)(2,1)}) custom-call(s32[1]{0:T(128)} %bitcast.slab_ref, f32[4]{0:T(128)} %weight_ref.3, s32[4]{0:T(128)} %offset_ref.3, bf16[4,2,128,128]{3,2,1,0:T(8,128)(2,1)} %previous_ref.3), custom_call_target="tpu_custom_call" | custom-call | tf_op jit(solution)/shard_map/partials/pallas_call | solution.py:211
  2.5 4.5 %collective-permute-start.2 = (bf16[2,2,128,128]{3,2,1,0:T(8,128)(2,1)}, bf16[2,2,128,128]{3,2,1,0:T(8,128)(2,1)S(1)}, u32[]{:S(2)}, u32[]{:S(2)}) collective-permute-start(bf16[2,2,128,128]{3,2,1,0:T(8,128)(2,1)} %get-tuple-element.18), channel_id=1, source_target_pairs={{0,1},{1,2},{2,3},{3,4},{4,5},{5,6},{6,7},{7,8},{8,9},{9,10},{10,1... | collective-permute-start | bytes 393224 | tf_op jit(solution)/shard_map/ppermute | solution.py:232
  7.0 4.4 %collective-permute-start.3 = (bf16[2,2,128,128]{3,2,1,0:T(8,128)(2,1)}, bf16[2,2,128,128]{3,2,1,0:T(8,128)(2,1)S(1)}, u32[]{:S(2)}, u32[]{:S(2)}) collective-permute-start(bf16[2,2,128,128]{3,2,1,0:T(8,128)(2,1)} %get-tuple-element.19), channel_id=1, source_target_pairs={{1,0},{2,1},{3,2},{4,3},{5,4},{6,5},{7,6},{8,7},{9,8},{10,9},{11,1... | collective-permute-start | bytes 393224 | tf_op jit(solution)/shard_map/ppermute | solution.py:233
  11.4 2.4 %collective-permute-start = (bf16[2,2,128,128]{3,2,1,0:T(8,128)(2,1)}, bf16[2,2,128,128]{3,2,1,0:T(8,128)(2,1)S(1)}, u32[]{:S(2)}, u32[]{:S(2)}) collective-permute-start(bf16[2,2,128,128]{3,2,1,0:T(8,128)(2,1)} %get-tuple-element.16), channel_id=1, source_target_pairs={{0,1},{1,2},{2,3},{3,4},{4,5},{5,6},{6,7},{7,8},{8,9},{9,10},{10,1... | collective-permute-start | bytes 393224 | tf_op jit(solution)/shard_map/ppermute | solution.py:234
  13.8 6.5 %collective-permute-start.1 = (bf16[2,2,128,128]{3,2,1,0:T(8,128)(2,1)}, bf16[2,2,128,128]{3,2,1,0:T(8,128)(2,1)S(1)}, u32[]{:S(2)}, u32[]{:S(2)}) collective-permute-start(bf16[2,2,128,128]{3,2,1,0:T(8,128)(2,1)} %get-tuple-element.17), channel_id=1, source_target_pairs={{1,0},{2,1},{3,2},{4,3},{5,4},{6,5},{7,6},{8,7},{9,8},{10,9},{11,1... | collective-permute-start | bytes 393224 | tf_op jit(solution)/shard_map/ppermute | solution.py:235
  20.3 2.4 %local.1 = (f32[4,2,128,128]{3,2,1,0:T(8,128)}, f32[4,2,128,128]{3,2,1,0:T(8,128)}, f32[4,2,128]{2,1,0:T(2,128)}, f32[128,128]{1,0:T(8,128)}) custom-call(s32[1]{0:T(128)} %bitcast.slab_ref, f32[4]{0:T(128)} %weight_ref.3, s32[4]{0:T(128)} %offset_ref.3, f32[4]{0:T(128)} %energy_ref.1, f32[128,128]{1,0:T(8,128)} %onsite_ref.1, ...), custom_call_target="tpu_custom_call" | custom-call | tf_op jit(solution)/shard_map/local/pallas_call | solution.py:211
  22.7 0.0 collective-permute-done.2.low_ref
  22.7 0.0 copy-start
  22.7 0.0 collective-permute-done.3.high_ref
  22.7 0.0 copy-start.1
  22.7 0.6 %copy-done = bf16[2,2,128,128]{3,2,1,0:T(8,128)(2,1)} copy-done((bf16[2,2,128,128]{3,2,1,0:T(8,128)(2,1)}, bf16[2,2,128,128]{3,2,1,0:T(8,128)(2,1)S(1)}, u32[]{:S(2)}) %copy-start) | copy-done | bytes 131096
  23.4 0.0 copy-done.1
  23.4 2.4 %first_tick.1 = (bf16[2,2,128,128]{3,2,1,0:T(8,128)(2,1)}, f32[2,2,128]{2,1,0:T(2,128)}) custom-call(s32[1]{0:T(128)} %bitcast.slab_ref, f32[4,2,128,128]{3,2,1,0:T(8,128)} %get-tuple-element.12.base_ref, f32[4,2,128,128]{3,2,1,0:T(8,128)} %get-tuple-element.13.product_ref, f32[4,2,128]{2,1,0:T(2,128)} %get-tuple-element.14.twice_ref, ...), custom_call_target="tpu_custom_call" | custom-call | tf_op jit(solution)/shard_map/first_tick/pallas_call | solution.py:211
  25.8 1.9 %collective-permute-start.4 = (bf16[2,2,128,128]{3,2,1,0:T(8,128)(2,1)}, bf16[2,2,128,128]{3,2,1,0:T(8,128)(2,1)S(1)}, u32[]{:S(2)}, u32[]{:S(2)}) collective-permute-start(bf16[2,2,128,128]{3,2,1,0:T(8,128)(2,1)} %get-tuple-element.20), channel_id=1, source_target_pairs={{0,16},{16,32},{32,48},{48,64},{64,80},{80,96},{96,112},{112,128},... | collective-permute-start | bytes 393224 | tf_op jit(solution)/shard_map/ppermute | solution.py:247
  27.7 0.0 collective-permute-done.low_ref
  27.7 0.0 copy-start.2
  27.7 0.0 collective-permute-done.1.high_ref
  27.7 0.0 copy-start.3
  27.7 17.3 %collective-permute-done.4.arriving_ref = bf16[2,2,128,128]{3,2,1,0:T(8,128)(2,1)S(1)} collective-permute-done((bf16[2,2,128,128]{3,2,1,0:T(8,128)(2,1)}, bf16[2,2,128,128]{3,2,1,0:T(8,128)(2,1)S(1)}, u32[]{:S(2)}, u32[]{:S(2)}) %collective-permute-start.4) | collective-permute-done | bytes 131104 | tf_op jit(solution)/shard_map/ppermute | solution.py:247
  45.0 0.0 copy-start.4
  45.0 0.0 copy-done.2
  45.0 0.0 copy-done.3
  45.1 0.6 %copy-done.4 = bf16[2,2,128,128]{3,2,1,0:T(8,128)(2,1)} copy-done((bf16[2,2,128,128]{3,2,1,0:T(8,128)(2,1)}, bf16[2,2,128,128]{3,2,1,0:T(8,128)(2,1)S(1)}, u32[]{:S(2)}) %copy-start.4) | copy-done | bytes 131096
  45.7 2.7 %last_tick.1 = (bf16[2,2,128,128]{3,2,1,0:T(8,128)(2,1)}, f32[4,2,128]{2,1,0:T(2,128)}) custom-call(s32[1]{0:T(128)} %bitcast.slab_ref, f32[4,2,128,128]{3,2,1,0:T(8,128)} %get-tuple-element.12.base_ref, f32[4,2,128,128]{3,2,1,0:T(8,128)} %get-tuple-element.13.product_ref, f32[4,2,128]{2,1,0:T(2,128)} %get-tuple-element.14.twice_ref, ...), custom_call_target="tpu_custom_call" | custom-call | tf_op jit(solution)/shard_map/last_tick/pallas_call | solution.py:211
Async XLA Ops:
  2.5 20.2 %collective-permute-start.2 = (bf16[2,2,128,128]{3,2,1,0:T(8,128)(2,1)}, bf16[2,2,128,128]{3,2,1,0:T(8,128)(2,1)S(1)}, u32[]{:S(2)}, u32[]{:S(2)}) collective-permute-start(bf16[2,2,128,128]{3,2,1,0:T(8,128)(2,1)} %get-tuple-element.18), channel_id=1, source_target_pairs={{0,1},{1,2},{2,3},{3,4},{4,5},{5,6},{6,7},{7,8},{8,9},{9,10},{10,1... | collective-permute-start | bytes 393224 | tf_op jit(solution)/shard_map/ppermute | solution.py:232
  7.0 15.7 %collective-permute-start.3 = (bf16[2,2,128,128]{3,2,1,0:T(8,128)(2,1)}, bf16[2,2,128,128]{3,2,1,0:T(8,128)(2,1)S(1)}, u32[]{:S(2)}, u32[]{:S(2)}) collective-permute-start(bf16[2,2,128,128]{3,2,1,0:T(8,128)(2,1)} %get-tuple-element.19), channel_id=1, source_target_pairs={{1,0},{2,1},{3,2},{4,3},{5,4},{6,5},{7,6},{8,7},{9,8},{10,9},{11,1... | collective-permute-start | bytes 393224 | tf_op jit(solution)/shard_map/ppermute | solution.py:233
  11.4 16.3 %collective-permute-start = (bf16[2,2,128,128]{3,2,1,0:T(8,128)(2,1)}, bf16[2,2,128,128]{3,2,1,0:T(8,128)(2,1)S(1)}, u32[]{:S(2)}, u32[]{:S(2)}) collective-permute-start(bf16[2,2,128,128]{3,2,1,0:T(8,128)(2,1)} %get-tuple-element.16), channel_id=1, source_target_pairs={{0,1},{1,2},{2,3},{3,4},{4,5},{5,6},{6,7},{7,8},{8,9},{9,10},{10,1... | collective-permute-start | bytes 393224 | tf_op jit(solution)/shard_map/ppermute | solution.py:234
  13.8 13.9 %collective-permute-start.1 = (bf16[2,2,128,128]{3,2,1,0:T(8,128)(2,1)}, bf16[2,2,128,128]{3,2,1,0:T(8,128)(2,1)S(1)}, u32[]{:S(2)}, u32[]{:S(2)}) collective-permute-start(bf16[2,2,128,128]{3,2,1,0:T(8,128)(2,1)} %get-tuple-element.17), channel_id=1, source_target_pairs={{1,0},{2,1},{3,2},{4,3},{5,4},{6,5},{7,6},{8,7},{9,8},{10,9},{11,1... | collective-permute-start | bytes 393224 | tf_op jit(solution)/shard_map/ppermute | solution.py:235
  22.7 0.7 %copy-start = (bf16[2,2,128,128]{3,2,1,0:T(8,128)(2,1)}, bf16[2,2,128,128]{3,2,1,0:T(8,128)(2,1)S(1)}, u32[]{:S(2)}) copy-start(bf16[2,2,128,128]{3,2,1,0:T(8,128)(2,1)S(1)} %collective-permute-done.2.low_ref) | copy-start | bytes 393220
  22.7 0.7 %copy-start.1 = (bf16[2,2,128,128]{3,2,1,0:T(8,128)(2,1)}, bf16[2,2,128,128]{3,2,1,0:T(8,128)(2,1)S(1)}, u32[]{:S(2)}) copy-start(bf16[2,2,128,128]{3,2,1,0:T(8,128)(2,1)S(1)} %collective-permute-done.3.high_ref) | copy-start | bytes 393220
  25.8 19.3 %collective-permute-start.4 = (bf16[2,2,128,128]{3,2,1,0:T(8,128)(2,1)}, bf16[2,2,128,128]{3,2,1,0:T(8,128)(2,1)S(1)}, u32[]{:S(2)}, u32[]{:S(2)}) collective-permute-start(bf16[2,2,128,128]{3,2,1,0:T(8,128)(2,1)} %get-tuple-element.20), channel_id=1, source_target_pairs={{0,16},{16,32},{32,48},{48,64},{64,80},{80,96},{96,112},{112,128},... | collective-permute-start | bytes 393224 | tf_op jit(solution)/shard_map/ppermute | solution.py:247
  27.7 17.3 %copy-start.2 = (bf16[2,2,128,128]{3,2,1,0:T(8,128)(2,1)}, bf16[2,2,128,128]{3,2,1,0:T(8,128)(2,1)S(1)}, u32[]{:S(2)}) copy-start(bf16[2,2,128,128]{3,2,1,0:T(8,128)(2,1)S(1)} %collective-permute-done.low_ref) | copy-start | bytes 393220
  27.7 17.3 %copy-start.3 = (bf16[2,2,128,128]{3,2,1,0:T(8,128)(2,1)}, bf16[2,2,128,128]{3,2,1,0:T(8,128)(2,1)S(1)}, u32[]{:S(2)}) copy-start(bf16[2,2,128,128]{3,2,1,0:T(8,128)(2,1)S(1)} %collective-permute-done.1.high_ref) | copy-start | bytes 393220
  45.0 0.6 %copy-start.4 = (bf16[2,2,128,128]{3,2,1,0:T(8,128)(2,1)}, bf16[2,2,128,128]{3,2,1,0:T(8,128)(2,1)S(1)}, u32[]{:S(2)}) copy-start(bf16[2,2,128,128]{3,2,1,0:T(8,128)(2,1)S(1)} %collective-permute-done.4.arriving_ref) | copy-start | bytes 393220

commit v2 on v1

--- a/solution.py
+++ b/solution.py
@@ -18,16 +18,17 @@
 bf16 = jnp.bfloat16
 
 VMEM = pltpu.MemorySpace.VMEM
-SMEM = pltpu.MemorySpace.SMEM
+
+
+def slab_parity():
+    return lax.axis_index("slab") & 1
 
 
 def offset_weights(weight_ref, offset_ref):
     sums = {}
     for distance in range(1, OMAX + 1):
-        total = jnp.float32(0.0)
-        for mode in range(MODES):
-            total = total + jnp.where(offset_ref[mode] == distance, weight_ref[mode], 0.0)
-        sums[distance] = total
+        hits = jnp.where(offset_ref[...] == distance, weight_ref[...], 0.0)
+        sums[distance] = jnp.sum(hits, axis=1, keepdims=True)
     return sums
 
 
@@ -39,29 +40,40 @@
     return total
 
 
-def partial_kernel(slab_ref, weight_ref, offset_ref, previous_ref, up0_ref, down0_ref, up1_ref, down1_ref):
-    sums = offset_weights(weight_ref, offset_ref)
-
-    def fill(ups, downs):
-        for part in range(2):
-            for row in range(0, B, CHUNK):
-                rows = pl.ds(row, CHUNK)
-                values = [previous_ref[e, part, rows, :].astype(f32) for e in range(E_DEV)]
-                for target in range(E_DEV):
-                    up = weighted([(sums[OMAX + target - e], values[e]) for e in range(target, E_DEV)])
-                    down = weighted([(sums[e + OMAX - target], values[e]) for e in range(0, target + 1)])
-                    ups[target // EB][target % EB, part, rows, :] = up.astype(bf16)
-                    downs[target // EB][target % EB, part, rows, :] = down.astype(bf16)
-
-    parity = slab_ref[0]
-
-    @pl.when(parity == 0)
-    def _():
-        fill((up0_ref, up1_ref), (down0_ref, down1_ref))
-
-    @pl.when(parity != 0)
-    def _():
-        fill((up1_ref, up0_ref), (down1_ref, down0_ref))
+def fill_partials(batch, sums, previous_ref, up_ref, down_ref):
+    for part in range(2):
+        for row in range(0, B, CHUNK):
+            rows = pl.ds(row, CHUNK)
+            values = [previous_ref[e, part, rows, :].astype(f32) for e in range(E_DEV)]
+            for m in range(EB):
+                target = batch * EB + m
+                up = weighted([(sums[OMAX + target - e], values[e]) for e in range(target, E_DEV)])
+                down = weighted([(sums[e + OMAX - target], values[e]) for e in range(0, target + 1)])
+                up_ref[m, part, rows, :] = up.astype(bf16)
+                down_ref[m, part, rows, :] = down.astype(bf16)
+
+
+def tick_partials(tick, sums, previous_ref, up_ref, down_ref):
+    parity = slab_parity()
+    for batch in range(2):
+
+        @pl.when(parity == (batch ^ tick))
+        def _():
+            fill_partials(batch, sums, previous_ref, up_ref, down_ref)
+
+
+def opening_kernel(*refs):
+    count = (len(refs) - 3) // 2
+    inputs, (up_ref, down_ref), kept, semaphores = refs[:count], refs[count : count + 2], refs[count + 2 : -1], refs[-1]
+    copies = [pltpu.make_async_copy(inputs[i], kept[i], semaphores.at[i]) for i in range(count)]
+    for copy in copies:
+        copy.start()
+    for copy in copies[:3]:
+        copy.wait()
+    previous_ref, weight_ref, offset_ref = kept[:3]
+    tick_partials(0, offset_weights(weight_ref, offset_ref), previous_ref, up_ref, down_ref)
+    for copy in copies[3:]:
+        copy.wait()
 
 
 def mixed_coupling(coupling, blocks):
@@ -77,10 +89,11 @@
 
 
 def local_kernel(
-    slab_ref, weight_ref, offset_ref, energy_ref, onsite_ref, coupling_ref, atom_ref, strength_ref,
-    previous_ref, flight_ref, base_ref, product_ref, twice_ref, pair_ref,
+    previous_ref, weight_ref, offset_ref, flight_ref, onsite_ref, coupling_ref, energy_ref, atom_ref, strength_ref,
+    up_ref, down_ref, base_ref, product_ref, twice_ref, pair_ref,
 ):
     sums = offset_weights(weight_ref, offset_ref)
+    tick_partials(1, sums, previous_ref, up_ref, down_ref)
     on_diagonal = diagonal_mask()
     atoms = lax.broadcasted_iota(jnp.int32, (ATOMS, ATOMS), 0) == lax.broadcasted_iota(jnp.int32, (ATOMS, ATOMS), 1)
     strength_column = jnp.sum(jnp.where(atoms, strength_ref[...], 0.0), axis=1, keepdims=True)
@@ -97,8 +110,8 @@
         return gap / denominator, -broadening / denominator
 
     for e in range(E_DEV):
-        row_real, row_imag = start(energy_ref[e] - level_row)
-        column_real, column_imag = start(energy_ref[e] - level_column)
+        row_real, row_imag = start(energy_ref[:, e : e + 1] - level_row)
+        column_real, column_imag = start(energy_ref[:, e : e + 1] - level_column)
         product_ref[e, 0] = column_real * row_real - column_imag * row_imag
         product_ref[e, 1] = column_real * row_imag + column_imag * row_real
         twice_ref[e, 0:1, :] = 2.0 * row_real
@@ -114,12 +127,12 @@
             for target in range(E_DEV):
                 phonon = weighted([(sums[abs(target - e)], values[e]) for e in range(E_DEV) if e != target])
                 if part == 0:
-                    head = jnp.where(mask, energy_ref[target], 0.0) - onsite
+                    head = jnp.where(mask, energy_ref[:, target : target + 1], 0.0) - onsite
                 else:
                     head = jnp.where(mask, jnp.float32(broadening), 0.0)
                 base_ref[target, part, rows, :] = head - phonon * pair
 
-    first = slab_ref[0] * EB
+    first = slab_parity() * EB
     coupled = mixed_coupling(coupling_ref[...], [flight_ref[m, c] for m in range(EB) for c in range(2)])
     for m in range(EB):
         for c in range(2):
@@ -158,8 +171,8 @@
     return jnp.sum(jnp.where(on_diagonal, green.astype(f32), 0.0), axis=0, keepdims=True)
 
 
-def first_tick_kernel(slab_ref, base_ref, product_ref, twice_ref, pair_ref, low_ref, high_ref, green_ref, diagonal_ref):
-    first = slab_ref[0] * EB
+def first_tick_kernel(base_ref, product_ref, twice_ref, pair_ref, low_ref, high_ref, green_ref, diagonal_ref):
+    first = slab_parity() * EB
     on_diagonal = diagonal_mask()
     pair = pair_ref[...]
     for m in range(EB):
@@ -177,11 +190,11 @@
 
 
 def last_tick_kernel(
-    slab_ref, base_ref, product_ref, twice_ref, pair_ref, low_ref, high_ref, arriving_ref, coupling_ref,
+    base_ref, product_ref, twice_ref, pair_ref, low_ref, high_ref, arriving_ref, coupling_ref,
     earlier_ref, green_ref, diagonal_ref,
 ):
-    earlier = slab_ref[0] * EB
-    first = (1 - slab_ref[0]) * EB
+    earlier = slab_parity() * EB
+    first = (1 - slab_parity()) * EB
     on_diagonal = diagonal_mask()
     pair = pair_ref[...]
     coupled = mixed_coupling(coupling_ref[...], [arriving_ref[m, c] for m in range(EB) for c in range(2)])
@@ -203,52 +216,57 @@
             diagonal_ref[e, c : c + 1, :] = green_diagonal(greens[c], on_diagonal)
 
 
-def spec(space):
-    return pl.BlockSpec(memory_space=space)
-
-
-def call(kernel, scalars, arrays, outs, name):
+def call(kernel, arrays, outs, name, kept=True):
+    arrays = [pltpu.with_memory_space_constraint(array, VMEM) for array in arrays]
+    shapes = [VMEM(shape, dtype) if kept else jax.ShapeDtypeStruct(shape, dtype) for shape, dtype in outs]
+    space = pl.BlockSpec(memory_space=VMEM)
     return pl.pallas_call(
         kernel,
-        in_specs=[spec(SMEM)] * len(scalars) + [spec(VMEM)] * len(arrays),
-        out_specs=[spec(VMEM)] * len(outs),
-        out_shape=[jax.ShapeDtypeStruct(shape, dtype) for shape, dtype in outs],
+        in_specs=[space] * len(arrays),
+        out_specs=[space] * len(outs),
+        out_shape=shapes,
         name=name,
-    )(*scalars, *arrays)
+    )(*arrays)
 
 
 def body(energy, onsite, coupling, atom_of, strength, previous, phonon_weight, offsets, in_flight):
-    parity = (lax.axis_index("slab") & 1).astype(jnp.int32).reshape(1)
     devices = lax.axis_size("energy")
     up = [(i, i + 1) for i in range(devices - 1)]
     down = [(i + 1, i) for i in range(devices - 1)]
     slabs = lax.axis_size("slab")
     onward = [(i, i + 1) for i in range(slabs - 1)]
     half = (EB, 2, B, B)
-
-    up0, down0, up1, down1 = call(
-        partial_kernel, (parity, phonon_weight, offsets), (previous,), [(half, bf16)] * 4, "partials"
-    )
+    arrays = (
+        previous, phonon_weight.reshape(1, MODES), offsets.reshape(1, MODES), in_flight, onsite, coupling,
+        energy.reshape(1, E_DEV), atom_of.reshape(1, B), strength.reshape(1, ATOMS),
+    )
+    up0, down0, *kept = pl.pallas_call(
+        opening_kernel,
+        in_specs=[pl.BlockSpec(memory_space=pl.ANY)] * len(arrays),
+        out_specs=[pl.BlockSpec(memory_space=VMEM)] * (len(arrays) + 2),
+        out_shape=[VMEM(half, bf16)] * 2 + [VMEM(array.shape, array.dtype) for array in arrays],
+        scratch_shapes=[pltpu.SemaphoreType.DMA((len(arrays),))],
+        name="opening",
+    )(*arrays)
     low0 = lax.ppermute(up0, "energy", up)
     high0 = lax.ppermute(down0, "energy", down)
+    up1, down1, base, product, twice, pair = call(
+        local_kernel,
+        kept,
+        [(half, bf16)] * 2
+        + [((E_DEV, 2, B, B), f32), ((E_DEV, 2, B, B), f32), ((E_DEV, 2, B), f32), ((B, B), f32)],
+        "local",
+    )
     low1 = lax.ppermute(up1, "energy", up)
     high1 = lax.ppermute(down1, "energy", down)
-    base, product, twice, pair = call(
-        local_kernel,
-        (parity, phonon_weight, offsets, energy),
-        (onsite, coupling, atom_of.reshape(1, B), strength.reshape(1, ATOMS), previous, in_flight),
-        [((E_DEV, 2, B, B), f32), ((E_DEV, 2, B, B), f32), ((E_DEV, 2, B), f32), ((B, B), f32)],
-        "local",
-    )
     green0, diagonal0 = call(
-        first_tick_kernel, (parity,), (base, product, twice, pair, low0, high0),
-        [(half, bf16), ((EB, 2, B), f32)], "first_tick",
+        first_tick_kernel, (base, product, twice, pair, low0, high0), [(half, bf16), ((EB, 2, B), f32)], "first_tick"
     )
     arriving = lax.ppermute(green0, "slab", onward)
     green1, diagonals = call(
-        last_tick_kernel, (parity,),
-        (base, product, twice, pair, low1, high1, arriving, coupling, diagonal0),
-        [(half, bf16), ((E_DEV, 2, B), f32)], "last_tick",
+        last_tick_kernel,
+        (base, product, twice, pair, low1, high1, arriving, kept[5], diagonal0),
+        [(half, bf16), ((E_DEV, 2, B), f32)], "last_tick", kept=False,
     )
     return green1, diagonals
 

time: 48.7 us -> 41.4 us (0.85)
  Pallas kernels: 9.42 us -> 3.72 us
  local copies, waits for them, and re-layouts: 1.32 us -> 0 us
    pallas_call x4, Pallas kernels: 9.42 us -> 3.72 us  [the longest x3 2.5 us: call(): pl.pallas_call(kernel, in_specs=[space] * len(arrays), out_specs=[space]...]
    ppermute x1, waiting for transfers between devices: 17.3 us -> 14.7 us  [body(): arriving = lax.ppermute(green0, 'slab', onward)]
    ppermute x1, waiting for transfers between devices: 0.01 us -> 1.35 us  [body(): high1 = lax.ppermute(down1, 'energy', down)]
    unnamed x10 -> x0, local copies, waits for them, and re-layouts: 1.32 us -> none
    ppermute x1, waiting for transfers between devices: 0.01 us -> 1.11 us  [body(): low1 = lax.ppermute(up1, 'energy', up)]
  transfers between devices with their start and end apart: 5 -> 5, of which waited for: 1 -> 3; matrix products, arithmetic and copies ran while one was open for 0% -> 0% of each run, Pallas kernels for 10% -> 3%
where the time goes in v2:
time: 41.4 us; the launch traced here: 41.2 us
  starting transfers between devices  19.6 us (47%)
  waiting for transfers between devices  17.2 us (42%)
  Pallas kernels  3.72 us (9%)
  between operations  0.71 us (2%)
    ppermute x1, waiting for transfers between devices, body(): arriving = lax.ppermute(green0, 'slab', onward)  14.7 us
    ppermute x1, starting transfers between devices, body(): high1 = lax.ppermute(down1, 'energy', down)  6.46 us
    ppermute x1, starting transfers between devices, body(): low0 = lax.ppermute(up0, 'energy', up)  4.5 us
    ppermute x1, starting transfers between devices, body(): high0 = lax.ppermute(down0, 'energy', down)  4.35 us
    pallas_call x3, Pallas kernels, call(): pl.pallas_call(kernel, in_specs=[space] * len(arrays), out_specs=[space]...  2.5 us
    ppermute x1, starting transfers between devices, body(): low1 = lax.ppermute(up1, 'energy', up)  2.39 us
    ppermute x1, starting transfers between devices, body(): arriving = lax.ppermute(green0, 'slab', onward)  1.92 us
    ppermute x1, waiting for transfers between devices, body(): high1 = lax.ppermute(down1, 'energy', down)  1.35 us
  transfers between devices with their start and end apart: 5, of which 3 were waited for; matrix products, arithmetic and copies ran while one was open for 0% of the time, Pallas kernels for 3%

profile of v2, /device:TPU:14, one launch (start us, length us, event | category | flops | bytes accessed | tf_op | source)
XLA Modules:
  0.0 41.2 jit_solution(564268222735660875)
XLA Ops:
  0.6 1.2 %opening.1 = (bf16[2,2,128,128]{3,2,1,0:T(8,128)(2,1)S(1)}, bf16[2,2,128,128]{3,2,1,0:T(8,128)(2,1)S(1)}, bf16[4,2,128,128]{3,2,1,0:T(8,128)(2,1)S(1)}, f32[1,4]...) custom-call(bf16[4,2,128,128]{3,2,1,0:T(8,128)(2,1)} %refs_0_.1, ...), custom_call_target="tpu_custom_call" | custom-call | tf_op jit(solution)/shard_map/opening/pallas_call | solution.py:243
  1.9 4.5 %collective-permute-start.2 = (bf16[2,2,128,128]{3,2,1,0:T(8,128)(2,1)S(1)}, bf16[2,2,128,128]{3,2,1,0:T(8,128)(2,1)S(1)}, u32[]{:S(2)}, u32[]{:S(2)}) collective-permute-start(bf16[2,2,128,128]{3,2,1,0:T(8,128)(2,1)S(1)} %get-tuple-element.36), channel_id=1, source_target_pairs={{0,1},{1,2},{2,3},{3,4},{4,5},{5,6},{6,7},{7,8},{8,9},{9,10},{10,1... | collective-permute-start | bytes 393224 | tf_op jit(solution)/shard_map/ppermute | solution.py:251
  6.4 4.4 %collective-permute-start.3 = (bf16[2,2,128,128]{3,2,1,0:T(8,128)(2,1)S(1)}, bf16[2,2,128,128]{3,2,1,0:T(8,128)(2,1)S(1)}, u32[]{:S(2)}, u32[]{:S(2)}) collective-permute-start(bf16[2,2,128,128]{3,2,1,0:T(8,128)(2,1)S(1)} %get-tuple-element.37), channel_id=1, source_target_pairs={{1,0},{2,1},{3,2},{4,3},{5,4},{6,5},{7,6},{8,7},{9,8},{10,9},{11,1... | collective-permute-start | bytes 393224 | tf_op jit(solution)/shard_map/ppermute | solution.py:252
  10.7 0.7 %local.1 = (bf16[2,2,128,128]{3,2,1,0:T(8,128)(2,1)S(1)}, bf16[2,2,128,128]{3,2,1,0:T(8,128)(2,1)S(1)}, f32[4,2,128,128]{3,2,1,0:T(8,128)S(1)}, f32[4,2,128,128]...) custom-call(bf16[4,2,128,128]{3,2,1,0:T(8,128)(2,1)S(1)} %get-tuple-element.21.previous_ref, ...), custom_call_target="tpu_custom_call" | custom-call | tf_op jit(solution)/shard_map/local/pallas_call | solution.py:223
  11.4 2.4 %collective-permute-start = (bf16[2,2,128,128]{3,2,1,0:T(8,128)(2,1)S(1)}, bf16[2,2,128,128]{3,2,1,0:T(8,128)(2,1)S(1)}, u32[]{:S(2)}, u32[]{:S(2)}) collective-permute-start(bf16[2,2,128,128]{3,2,1,0:T(8,128)(2,1)S(1)} %get-tuple-element.34), channel_id=1, source_target_pairs={{0,1},{1,2},{2,3},{3,4},{4,5},{5,6},{6,7},{7,8},{8,9},{9,10},{10,1... | collective-permute-start | bytes 393224 | tf_op jit(solution)/shard_map/ppermute | solution.py:260
  13.8 6.5 %collective-permute-start.1 = (bf16[2,2,128,128]{3,2,1,0:T(8,128)(2,1)S(1)}, bf16[2,2,128,128]{3,2,1,0:T(8,128)(2,1)S(1)}, u32[]{:S(2)}, u32[]{:S(2)}) collective-permute-start(bf16[2,2,128,128]{3,2,1,0:T(8,128)(2,1)S(1)} %get-tuple-element.35), channel_id=1, source_target_pairs={{1,0},{2,1},{3,2},{4,3},{5,4},{6,5},{7,6},{8,7},{9,8},{10,9},{11,1... | collective-permute-start | bytes 393224 | tf_op jit(solution)/shard_map/ppermute | solution.py:261
  20.3 0.0 collective-permute-done.2.low_ref
  20.3 0.0 collective-permute-done.3.high_ref
  20.3 0.4 %first_tick.1 = (bf16[2,2,128,128]{3,2,1,0:T(8,128)(2,1)S(1)}, f32[2,2,128]{2,1,0:T(2,128)S(1)}) custom-call(f32[4,2,128,128]{3,2,1,0:T(8,128)S(1)} %get-tuple-element.30.base_ref, f32[4,2,128,128]{3,2,1,0:T(8,128)S(1)} %get-tuple-element.31.product_ref, f32[4,2,128]{2,1,0:T(2,128)S(1)} %get-tuple-element.32.twice_ref, ...), custom_call_target="tpu_custom_call" | custom-call | tf_op jit(solution)/shard_map/first_tick/pallas_call | solution.py:223
  20.8 1.9 %collective-permute-start.4 = (bf16[2,2,128,128]{3,2,1,0:T(8,128)(2,1)S(1)}, bf16[2,2,128,128]{3,2,1,0:T(8,128)(2,1)S(1)}, u32[]{:S(2)}, u32[]{:S(2)}) collective-permute-start(bf16[2,2,128,128]{3,2,1,0:T(8,128)(2,1)S(1)} %get-tuple-element.38), channel_id=1, source_target_pairs={{0,16},{16,32},{32,48},{48,64},{64,80},{80,96},{96,112},{112,128},... | collective-permute-start | bytes 393224 | tf_op jit(solution)/shard_map/ppermute | solution.py:265
  22.7 1.1 %collective-permute-done.low_ref = bf16[2,2,128,128]{3,2,1,0:T(8,128)(2,1)S(1)} collective-permute-done((bf16[2,2,128,128]{3,2,1,0:T(8,128)(2,1)S(1)}, bf16[2,2,128,128]{3,2,1,0:T(8,128)(2,1)S(1)}, u32[]{:S(2)}, u32[]{:S(2)}) %collective-permute-start) | collective-permute-done | bytes 131104 | tf_op jit(solution)/shard_map/ppermute | solution.py:260
  23.8 1.4 %collective-permute-done.1.high_ref = bf16[2,2,128,128]{3,2,1,0:T(8,128)(2,1)S(1)} collective-permute-done((bf16[2,2,128,128]{3,2,1,0:T(8,128)(2,1)S(1)}, bf16[2,2,128,128]{3,2,1,0:T(8,128)(2,1)S(1)}, u32[]{:S(2)}, u32[]{:S(2)}) %collective-permute-start.1) | collective-permute-done | bytes 131104 | tf_op jit(solution)/shard_map/ppermute | solution.py:261
  25.1 14.7 %collective-permute-done.4.arriving_ref = bf16[2,2,128,128]{3,2,1,0:T(8,128)(2,1)S(1)} collective-permute-done((bf16[2,2,128,128]{3,2,1,0:T(8,128)(2,1)S(1)}, bf16[2,2,128,128]{3,2,1,0:T(8,128)(2,1)S(1)}, u32[]{:S(2)}, u32[]{:S(2)}) %collective-permute-start.4) | collective-permute-done | bytes 131104 | tf_op jit(solution)/shard_map/ppermute | solution.py:265
  39.8 1.4 %last_tick.1 = (bf16[2,2,128,128]{3,2,1,0:T(8,128)(2,1)}, f32[4,2,128]{2,1,0:T(2,128)}) custom-call(f32[4,2,128,128]{3,2,1,0:T(8,128)S(1)} %get-tuple-element.30.base_ref, f32[4,2,128,128]{3,2,1,0:T(8,128)S(1)} %get-tuple-element.31.product_ref, f32[4,2,128]{2,1,0:T(2,128)S(1)} %get-tuple-element.32.twice_ref, f32[128,128]{1,0:T(8,128)S(1)} %get-tuple-element.33.pair_ref, ...), custom_call_target="tpu_custom_call" | custom-call | tf_op jit(solution)/shard_map/last_tick/pallas_call | solution.py:223
Async XLA Ops:
  1.9 18.4 %collective-permute-start.2 = (bf16[2,2,128,128]{3,2,1,0:T(8,128)(2,1)S(1)}, bf16[2,2,128,128]{3,2,1,0:T(8,128)(2,1)S(1)}, u32[]{:S(2)}, u32[]{:S(2)}) collective-permute-start(bf16[2,2,128,128]{3,2,1,0:T(8,128)(2,1)S(1)} %get-tuple-element.36), channel_id=1, source_target_pairs={{0,1},{1,2},{2,3},{3,4},{4,5},{5,6},{6,7},{7,8},{8,9},{9,10},{10,1... | collective-permute-start | bytes 393224 | tf_op jit(solution)/shard_map/ppermute | solution.py:251
  6.4 13.9 %collective-permute-start.3 = (bf16[2,2,128,128]{3,2,1,0:T(8,128)(2,1)S(1)}, bf16[2,2,128,128]{3,2,1,0:T(8,128)(2,1)S(1)}, u32[]{:S(2)}, u32[]{:S(2)}) collective-permute-start(bf16[2,2,128,128]{3,2,1,0:T(8,128)(2,1)S(1)} %get-tuple-element.37), channel_id=1, source_target_pairs={{1,0},{2,1},{3,2},{4,3},{5,4},{6,5},{7,6},{8,7},{9,8},{10,9},{11,1... | collective-permute-start | bytes 393224 | tf_op jit(solution)/shard_map/ppermute | solution.py:252
  11.4 12.4 %collective-permute-start = (bf16[2,2,128,128]{3,2,1,0:T(8,128)(2,1)S(1)}, bf16[2,2,128,128]{3,2,1,0:T(8,128)(2,1)S(1)}, u32[]{:S(2)}, u32[]{:S(2)}) collective-permute-start(bf16[2,2,128,128]{3,2,1,0:T(8,128)(2,1)S(1)} %get-tuple-element.34), channel_id=1, source_target_pairs={{0,1},{1,2},{2,3},{3,4},{4,5},{5,6},{6,7},{7,8},{8,9},{9,10},{10,1... | collective-permute-start | bytes 393224 | tf_op jit(solution)/shard_map/ppermute | solution.py:260
  13.8 11.3 %collective-permute-start.1 = (bf16[2,2,128,128]{3,2,1,0:T(8,128)(2,1)S(1)}, bf16[2,2,128,128]{3,2,1,0:T(8,128)(2,1)S(1)}, u32[]{:S(2)}, u32[]{:S(2)}) collective-permute-start(bf16[2,2,128,128]{3,2,1,0:T(8,128)(2,1)S(1)} %get-tuple-element.35), channel_id=1, source_target_pairs={{1,0},{2,1},{3,2},{4,3},{5,4},{6,5},{7,6},{8,7},{9,8},{10,9},{11,1... | collective-permute-start | bytes 393224 | tf_op jit(solution)/shard_map/ppermute | solution.py:261
  20.8 19.1 %collective-permute-start.4 = (bf16[2,2,128,128]{3,2,1,0:T(8,128)(2,1)S(1)}, bf16[2,2,128,128]{3,2,1,0:T(8,128)(2,1)S(1)}, u32[]{:S(2)}, u32[]{:S(2)}) collective-permute-start(bf16[2,2,128,128]{3,2,1,0:T(8,128)(2,1)S(1)} %get-tuple-element.38), channel_id=1, source_target_pairs={{0,16},{16,32},{32,48},{48,64},{64,80},{80,96},{96,112},{112,128},... | collective-permute-start | bytes 393224 | tf_op jit(solution)/shard_map/ppermute | solution.py:265

commit v3 on v2

--- a/solution.py
+++ b/solution.py
@@ -1,3 +1,5 @@
+import functools
+
 import jax
 import jax.numpy as jnp
 from jax import lax
@@ -63,15 +65,17 @@
 
 
 def opening_kernel(*refs):
-    count = (len(refs) - 3) // 2
-    inputs, (up_ref, down_ref), kept, semaphores = refs[:count], refs[count : count + 2], refs[count + 2 : -1], refs[-1]
+    count = (len(refs) - 5) // 2
+    inputs, outs, kept, semaphores = refs[:count], refs[count : count + 4], refs[count + 4 : -1], refs[-1]
     copies = [pltpu.make_async_copy(inputs[i], kept[i], semaphores.at[i]) for i in range(count)]
     for copy in copies:
         copy.start()
     for copy in copies[:3]:
         copy.wait()
     previous_ref, weight_ref, offset_ref = kept[:3]
-    tick_partials(0, offset_weights(weight_ref, offset_ref), previous_ref, up_ref, down_ref)
+    sums = offset_weights(weight_ref, offset_ref)
+    for tick in range(2):
+        tick_partials(tick, sums, previous_ref, outs[2 * tick], outs[2 * tick + 1])
     for copy in copies[3:]:
         copy.wait()
 
@@ -90,10 +94,9 @@
 
 def local_kernel(
     previous_ref, weight_ref, offset_ref, flight_ref, onsite_ref, coupling_ref, energy_ref, atom_ref, strength_ref,
-    up_ref, down_ref, base_ref, product_ref, twice_ref, pair_ref,
+    base_ref, product_ref, twice_ref, pair_ref,
 ):
     sums = offset_weights(weight_ref, offset_ref)
-    tick_partials(1, sums, previous_ref, up_ref, down_ref)
     on_diagonal = diagonal_mask()
     atoms = lax.broadcasted_iota(jnp.int32, (ATOMS, ATOMS), 0) == lax.broadcasted_iota(jnp.int32, (ATOMS, ATOMS), 1)
     strength_column = jnp.sum(jnp.where(atoms, strength_ref[...], 0.0), axis=1, keepdims=True)
@@ -171,14 +174,26 @@
     return jnp.sum(jnp.where(on_diagonal, green.astype(f32), 0.0), axis=0, keepdims=True)
 
 
-def first_tick_kernel(base_ref, product_ref, twice_ref, pair_ref, low_ref, high_ref, green_ref, diagonal_ref):
+def halo_sum(refs, m, c):
+    total = None
+    for ref, index in refs:
+        value = ref[index + (m, c)].astype(f32)
+        total = value if total is None else total + value
+    return total
+
+
+def first_tick_kernel(indices, *refs):
+    base_ref, product_ref, twice_ref, pair_ref = refs[:4]
+    halos = list(zip(refs[4:-2], indices))
+    green_ref, diagonal_ref = refs[-2:]
+
     first = slab_parity() * EB
     on_diagonal = diagonal_mask()
     pair = pair_ref[...]
     for m in range(EB):
         e = first + m
         system = [
-            base_ref[e, c] - (low_ref[m, c].astype(f32) + high_ref[m, c].astype(f32)) * pair for c in range(2)
+            base_ref[e, c] - halo_sum(halos, m, c) * pair for c in range(2)
         ]
         greens = green_of(
             system[0], system[1], product_ref[e, 0], product_ref[e, 1],
@@ -189,10 +204,10 @@
             diagonal_ref[m, c : c + 1, :] = green_diagonal(greens[c], on_diagonal)
 
 
-def last_tick_kernel(
-    base_ref, product_ref, twice_ref, pair_ref, low_ref, high_ref, arriving_ref, coupling_ref,
-    earlier_ref, green_ref, diagonal_ref,
-):
+def last_tick_kernel(indices, *refs):
+    base_ref, product_ref, twice_ref, pair_ref = refs[:4]
+    halos = list(zip(refs[4:-5], indices))
+    arriving_ref, coupling_ref, earlier_ref, green_ref, diagonal_ref = refs[-5:]
     earlier = slab_parity() * EB
     first = (1 - slab_parity()) * EB
     on_diagonal = diagonal_mask()
@@ -202,7 +217,7 @@
         e = first + m
         system = [
             base_ref[e, c]
-            - (low_ref[m, c].astype(f32) + high_ref[m, c].astype(f32)) * pair
+            - halo_sum(halos, m, c) * pair
             - coupled[m * 2 + c]
             for c in range(2)
         ]
@@ -216,23 +231,17 @@
             diagonal_ref[e, c : c + 1, :] = green_diagonal(greens[c], on_diagonal)
 
 
-def call(kernel, arrays, outs, name, kept=True):
+def call(kernel, arrays, outs, kept=True):
     arrays = [pltpu.with_memory_space_constraint(array, VMEM) for array in arrays]
     shapes = [VMEM(shape, dtype) if kept else jax.ShapeDtypeStruct(shape, dtype) for shape, dtype in outs]
     space = pl.BlockSpec(memory_space=VMEM)
     return pl.pallas_call(
-        kernel,
-        in_specs=[space] * len(arrays),
-        out_specs=[space] * len(outs),
-        out_shape=shapes,
-        name=name,
+        kernel, in_specs=[space] * len(arrays), out_specs=[space] * len(outs), out_shape=shapes
     )(*arrays)
 
 
 def body(energy, onsite, coupling, atom_of, strength, previous, phonon_weight, offsets, in_flight):
     devices = lax.axis_size("energy")
-    up = [(i, i + 1) for i in range(devices - 1)]
-    down = [(i + 1, i) for i in range(devices - 1)]
     slabs = lax.axis_size("slab")
     onward = [(i, i + 1) for i in range(slabs - 1)]
     half = (EB, 2, B, B)
@@ -240,34 +249,68 @@
         previous, phonon_weight.reshape(1, MODES), offsets.reshape(1, MODES), in_flight, onsite, coupling,
         energy.reshape(1, E_DEV), atom_of.reshape(1, B), strength.reshape(1, ATOMS),
     )
-    up0, down0, *kept = pl.pallas_call(
+    up0, down0, up1, down1, *kept = pl.pallas_call(
         opening_kernel,
         in_specs=[pl.BlockSpec(memory_space=pl.ANY)] * len(arrays),
-        out_specs=[pl.BlockSpec(memory_space=VMEM)] * (len(arrays) + 2),
-        out_shape=[VMEM(half, bf16)] * 2 + [VMEM(array.shape, array.dtype) for array in arrays],
+        out_specs=[pl.BlockSpec(memory_space=VMEM)] * (len(arrays) + 4),
+        out_shape=[VMEM(half, bf16)] * 4 + [VMEM(array.shape, array.dtype) for array in arrays],
         scratch_shapes=[pltpu.SemaphoreType.DMA((len(arrays),))],
         name="opening",
     )(*arrays)
-    low0 = lax.ppermute(up0, "energy", up)
-    high0 = lax.ppermute(down0, "energy", down)
-    up1, down1, base, product, twice, pair = call(
-        local_kernel,
-        kept,
-        [(half, bf16)] * 2
-        + [((E_DEV, 2, B, B), f32), ((E_DEV, 2, B, B), f32), ((E_DEV, 2, B), f32), ((B, B), f32)],
-        "local",
-    )
-    low1 = lax.ppermute(up1, "energy", up)
-    high1 = lax.ppermute(down1, "energy", down)
-    green0, diagonal0 = call(
-        first_tick_kernel, (base, product, twice, pair, low0, high0), [(half, bf16), ((EB, 2, B), f32)], "first_tick"
-    )
-    arriving = lax.ppermute(green0, "slab", onward)
-    green1, diagonals = call(
-        last_tick_kernel,
-        (base, product, twice, pair, low1, high1, arriving, kept[5], diagonal0),
-        [(half, bf16), ((E_DEV, 2, B), f32)], "last_tick", kept=False,
-    )
+    energies = devices
+
+    def halo_pairs(step, chosen):
+        return [
+            (s * energies + j, s * energies + j + step)
+            for s in range(slabs)
+            if chosen(s)
+            for j in range(energies)
+            if 0 <= j + step < energies
+        ]
+
+    last = slabs // 2 - 1
+
+    def exchange(up_block, down_block, chosen):
+        both = ("slab", "energy")
+        low = lax.ppermute(up_block, both, halo_pairs(1, chosen))
+        high = lax.ppermute(down_block, both, halo_pairs(-1, chosen))
+        return low, high
+
+    def send_onward(block):
+        return lax.ppermute(block, "slab", onward)
+
+    def is_last(s):
+        return s == last
+
+    def is_other(s):
+        return s != last
+
+    def local_work():
+        return call(
+            local_kernel, kept,
+            [((E_DEV, 2, B, B), f32), ((E_DEV, 2, B, B), f32), ((E_DEV, 2, B), f32), ((B, B), f32)],
+        )
+
+    def first_tick(local, halos):
+        arrays, indices = zip(*halos)
+        return call(functools.partial(first_tick_kernel, indices), (*local, *arrays), [(half, bf16), ((EB, 2, B), f32)])
+
+    def last_tick(local, halos, arriving):
+        arrays, indices = zip(*halos)
+        return call(
+            functools.partial(last_tick_kernel, indices), (*local, *arrays, arriving, kept[5], diagonal0),
+            [(half, bf16), ((E_DEV, 2, B), f32)], kept=False,
+        )
+
+    a = exchange(up0, down0, is_last)
+    b = exchange(up0, down0, is_other)
+    local = local_work()
+    b1 = exchange(up1, down1, is_other)
+    green0, diagonal0 = first_tick(local, [(x, ()) for x in a + b])
+    arriving = send_onward(green0)
+    c1 = exchange(up1, down1, is_last)
+    late = [(x, ()) for x in b1 + c1]
+    green1, diagonals = last_tick(local, late, arriving)
     return green1, diagonals
 
 
@@ -283,6 +326,7 @@
         P(),
         P("energy", None, "slab", None),
     )
+
     return jax.shard_map(
         body,
         mesh=mesh,

time: 41.4 us -> 44.8 us (1.082)
  the two profiles are of different devices: /device:TPU:14 before, /device:TPU:44 now
where the time goes in v3:
time: 44.8 us; the launch traced here: 44.5 us
  starting transfers between devices  20.5 us (46%)
  waiting for transfers between devices  19.5 us (44%)
  Pallas kernels  3.68 us (8%)
  between operations  0.77 us (2%)
    ppermute x1, waiting for transfers between devices, send_onward(): return lax.ppermute(block, 'slab', onward)  18.3 us
    ppermute x4, starting transfers between devices, exchange(): high = lax.ppermute(down_block, both, halo_pairs(-1, chosen))  12.6 us
    ppermute x4, starting transfers between devices, exchange(): low = lax.ppermute(up_block, both, halo_pairs(1, chosen))  5.96 us
    pallas_call x3, Pallas kernels, call(): pl.pallas_call(kernel, in_specs=[space] * len(arrays), out_specs=[space]...  2.37 us
    ppermute x1, starting transfers between devices, send_onward(): return lax.ppermute(block, 'slab', onward)  1.92 us
    pallas_call x1, Pallas kernels, body(): pl.pallas_call(opening_kernel, in_specs=[pl.BlockSpec(memory_space=pl.ANY...  1.31 us
    ppermute x4, waiting for transfers between devices, exchange(): high = lax.ppermute(down_block, both, halo_pairs(-1, chosen))  1.18 us
  transfers between devices with their start and end apart: 9, of which 2 were waited for; matrix products, arithmetic and copies ran while one was open for 0% of the time, Pallas kernels for 2%

profile of v3, /device:TPU:44, one launch (start us, length us, event | category | flops | bytes accessed | tf_op | source)
XLA Modules:
  0.0 44.5 jit_solution(17462528822376422017)
XLA Ops:
  0.6 1.3 %opening.1 = (bf16[2,2,128,128]{3,2,1,0:T(8,128)(2,1)S(1)}, bf16[2,2,128,128]{3,2,1,0:T(8,128)(2,1)S(1)}, bf16[2,2,128,128]{3,2,1,0:T(8,128)(2,1)S(1)}, bf16[2,2...) custom-call(bf16[4,2,128,128]{3,2,1,0:T(8,128)(2,1)} %refs_0_.1, ...), custom_call_target="tpu_custom_call" | custom-call | tf_op jit(solution)/shard_map/opening/pallas_call | solution.py:252
  1.9 0.7 %collective-permute-start.4 = (bf16[2,2,128,128]{3,2,1,0:T(8,128)(2,1)S(1)}, bf16[2,2,128,128]{3,2,1,0:T(8,128)(2,1)S(1)}, u32[]{:S(2)}, u32[]{:S(2)}) collective-permute-start(bf16[2,2,128,128]{3,2,1,0:T(8,128)(2,1)S(1)} %get-tuple-element.36), channel_id=1, source_target_pairs={{496,497},{497,498},{498,499},{499,500},{500,501},{501,502},{502,5... | collective-permute-start | bytes 393224 | tf_op jit(solution)/shard_map/ppermute | solution.py:275
  2.6 0.7 %collective-permute-start.5 = (bf16[2,2,128,128]{3,2,1,0:T(8,128)(2,1)S(1)}, bf16[2,2,128,128]{3,2,1,0:T(8,128)(2,1)S(1)}, u32[]{:S(2)}, u32[]{:S(2)}) collective-permute-start(bf16[2,2,128,128]{3,2,1,0:T(8,128)(2,1)S(1)} %get-tuple-element.37), channel_id=1, source_target_pairs={{497,496},{498,497},{499,498},{500,499},{501,500},{502,501},{503,5... | collective-permute-start | bytes 393224 | tf_op jit(solution)/shard_map/ppermute | solution.py:276
  3.3 2.7 %collective-permute-start.6 = (bf16[2,2,128,128]{3,2,1,0:T(8,128)(2,1)S(1)}, bf16[2,2,128,128]{3,2,1,0:T(8,128)(2,1)S(1)}, u32[]{:S(2)}, u32[]{:S(2)}) collective-permute-start(bf16[2,2,128,128]{3,2,1,0:T(8,128)(2,1)S(1)} %get-tuple-element.36), channel_id=1, source_target_pairs={{0,1},{1,2},{2,3},{3,4},{4,5},{5,6},{6,7},{7,8},{8,9},{9,10},{10,1... | collective-permute-start | bytes 393224 | tf_op jit(solution)/shard_map/ppermute | solution.py:275
  6.0 5.3 %collective-permute-start.7 = (bf16[2,2,128,128]{3,2,1,0:T(8,128)(2,1)S(1)}, bf16[2,2,128,128]{3,2,1,0:T(8,128)(2,1)S(1)}, u32[]{:S(2)}, u32[]{:S(2)}) collective-permute-start(bf16[2,2,128,128]{3,2,1,0:T(8,128)(2,1)S(1)} %get-tuple-element.37), channel_id=1, source_target_pairs={{1,0},{2,1},{3,2},{4,3},{5,4},{6,5},{7,6},{8,7},{9,8},{10,9},{11,1... | collective-permute-start | bytes 393224 | tf_op jit(solution)/shard_map/ppermute | solution.py:276
  11.3 1.9 %collective-permute-start = (bf16[2,2,128,128]{3,2,1,0:T(8,128)(2,1)S(1)}, bf16[2,2,128,128]{3,2,1,0:T(8,128)(2,1)S(1)}, u32[]{:S(2)}, u32[]{:S(2)}) collective-permute-start(bf16[2,2,128,128]{3,2,1,0:T(8,128)(2,1)S(1)} %get-tuple-element.34), channel_id=1, source_target_pairs={{0,1},{1,2},{2,3},{3,4},{4,5},{5,6},{6,7},{7,8},{8,9},{9,10},{10,1... | collective-permute-start | bytes 393224 | tf_op jit(solution)/shard_map/ppermute | solution.py:275
  13.2 0.5 %shard_map.104 = (f32[4,2,128,128]{3,2,1,0:T(8,128)S(1)}, f32[4,2,128,128]{3,2,1,0:T(8,128)S(1)}, f32[4,2,128]{2,1,0:T(2,128)S(1)}, f32[128,128]{1,0:T(8,128)S(1)}) custom-call(bf16[4,2,128,128]{3,2,1,0:T(8,128)(2,1)S(1)} %get-tuple-element.21.previous_ref, f32[1,4]{1,0:T(1,128)S(1)} %get-tuple-element.22.weight_ref, ...), custom_call_target="tpu_custom_call" | custom-call | tf_op jit(solution)/shard_map/pallas_call | solution.py:238
  13.7 0.0 collective-permute-done.4.refs_4_
  13.7 0.7 %collective-permute-start.2 = (bf16[2,2,128,128]{3,2,1,0:T(8,128)(2,1)S(1)}, bf16[2,2,128,128]{3,2,1,0:T(8,128)(2,1)S(1)}, u32[]{:S(2)}, u32[]{:S(2)}) collective-permute-start(bf16[2,2,128,128]{3,2,1,0:T(8,128)(2,1)S(1)} %get-tuple-element.34), channel_id=1, source_target_pairs={{496,497},{497,498},{498,499},{499,500},{500,501},{501,502},{502,5... | collective-permute-start | bytes 393224 | tf_op jit(solution)/shard_map/ppermute | solution.py:275
  14.4 0.0 collective-permute-done.5.refs_5_
  14.4 6.0 %collective-permute-start.1 = (bf16[2,2,128,128]{3,2,1,0:T(8,128)(2,1)S(1)}, bf16[2,2,128,128]{3,2,1,0:T(8,128)(2,1)S(1)}, u32[]{:S(2)}, u32[]{:S(2)}) collective-permute-start(bf16[2,2,128,128]{3,2,1,0:T(8,128)(2,1)S(1)} %get-tuple-element.35), channel_id=1, source_target_pairs={{1,0},{2,1},{3,2},{4,3},{5,4},{6,5},{7,6},{8,7},{9,8},{10,9},{11,1... | collective-permute-start | bytes 393224 | tf_op jit(solution)/shard_map/ppermute | solution.py:276
  20.4 0.0 collective-permute-done.6.refs_6_
  20.5 0.7 %collective-permute-start.3 = (bf16[2,2,128,128]{3,2,1,0:T(8,128)(2,1)S(1)}, bf16[2,2,128,128]{3,2,1,0:T(8,128)(2,1)S(1)}, u32[]{:S(2)}, u32[]{:S(2)}) collective-permute-start(bf16[2,2,128,128]{3,2,1,0:T(8,128)(2,1)S(1)} %get-tuple-element.35), channel_id=1, source_target_pairs={{497,496},{498,497},{499,498},{500,499},{501,500},{502,501},{503,5... | collective-permute-start | bytes 393224 | tf_op jit(solution)/shard_map/ppermute | solution.py:276
  21.1 0.0 collective-permute-done.7.refs_7_
  21.1 0.5 %shard_map.105 = (bf16[2,2,128,128]{3,2,1,0:T(8,128)(2,1)S(1)}, f32[2,2,128]{2,1,0:T(2,128)S(1)}) custom-call(f32[4,2,128,128]{3,2,1,0:T(8,128)S(1)} %get-tuple-element.30.refs_0_, f32[4,2,128,128]{3,2,1,0:T(8,128)S(1)} %get-tuple-element.31.refs_1_, f32[4,2,128]{2,1,0:T(2,128)S(1)} %get-tuple-element.32.refs_2_, f32[128,128]{1,0:T(8,128)S(1)} %get-tuple-element.33.refs_3_, ...), custom_call_target="tpu_custom_call" | custom-call | tf_op jit(solution)/shard_map/pallas_call | solution.py:238
  21.6 1.9 %collective-permute-start.8 = (bf16[2,2,128,128]{3,2,1,0:T(8,128)(2,1)S(1)}, bf16[2,2,128,128]{3,2,1,0:T(8,128)(2,1)S(1)}, u32[]{:S(2)}, u32[]{:S(2)}) collective-permute-start(bf16[2,2,128,128]{3,2,1,0:T(8,128)(2,1)S(1)} %get-tuple-element.38), channel_id=1, source_target_pairs={{0,16},{16,32},{32,48},{48,64},{64,80},{80,96},{96,112},{112,128},... | collective-permute-start | bytes 393224 | tf_op jit(solution)/shard_map/ppermute | solution.py:280
  23.6 0.0 collective-permute-done.refs_4_
  23.6 1.2 %collective-permute-done.1.refs_5_ = bf16[2,2,128,128]{3,2,1,0:T(8,128)(2,1)S(1)} collective-permute-done((bf16[2,2,128,128]{3,2,1,0:T(8,128)(2,1)S(1)}, bf16[2,2,128,128]{3,2,1,0:T(8,128)(2,1)S(1)}, u32[]{:S(2)}, u32[]{:S(2)}) %collective-permute-start.1) | collective-permute-done | bytes 131104 | tf_op jit(solution)/shard_map/ppermute | solution.py:276
  24.8 0.0 collective-permute-done.2.refs_6_
  24.8 0.0 collective-permute-done.3.refs_7_
  24.8 18.3 %collective-permute-done.8.refs_8_ = bf16[2,2,128,128]{3,2,1,0:T(8,128)(2,1)S(1)} collective-permute-done((bf16[2,2,128,128]{3,2,1,0:T(8,128)(2,1)S(1)}, bf16[2,2,128,128]{3,2,1,0:T(8,128)(2,1)S(1)}, u32[]{:S(2)}, u32[]{:S(2)}) %collective-permute-start.8) | collective-permute-done | bytes 131104 | tf_op jit(solution)/shard_map/ppermute | solution.py:280
  43.1 1.4 %shard_map.106 = (bf16[2,2,128,128]{3,2,1,0:T(8,128)(2,1)}, f32[4,2,128]{2,1,0:T(2,128)}) custom-call(f32[4,2,128,128]{3,2,1,0:T(8,128)S(1)} %get-tuple-element.30.refs_0_, f32[4,2,128,128]{3,2,1,0:T(8,128)S(1)} %get-tuple-element.31.refs_1_, f32[4,2,128]{2,1,0:T(2,128)S(1)} %get-tuple-element.32.refs_2_, f32[128,128]{1,0:T(8,128)S(1)} %get-tuple-element.33.refs_3_, ...), custom_call_target="tpu_custom_call" | custom-call | tf_op jit(solution)/shard_map/pallas_call | solution.py:238
Async XLA Ops:
  1.9 11.8 %collective-permute-start.4 = (bf16[2,2,128,128]{3,2,1,0:T(8,128)(2,1)S(1)}, bf16[2,2,128,128]{3,2,1,0:T(8,128)(2,1)S(1)}, u32[]{:S(2)}, u32[]{:S(2)}) collective-permute-start(bf16[2,2,128,128]{3,2,1,0:T(8,128)(2,1)S(1)} %get-tuple-element.36), channel_id=1, source_target_pairs={{496,497},{497,498},{498,499},{499,500},{500,501},{501,502},{502,5... | collective-permute-start | bytes 393224 | tf_op jit(solution)/shard_map/ppermute | solution.py:275
  2.6 11.8 %collective-permute-start.5 = (bf16[2,2,128,128]{3,2,1,0:T(8,128)(2,1)S(1)}, bf16[2,2,128,128]{3,2,1,0:T(8,128)(2,1)S(1)}, u32[]{:S(2)}, u32[]{:S(2)}) collective-permute-start(bf16[2,2,128,128]{3,2,1,0:T(8,128)(2,1)S(1)} %get-tuple-element.37), channel_id=1, source_target_pairs={{497,496},{498,497},{499,498},{500,499},{501,500},{502,501},{503,5... | collective-permute-start | bytes 393224 | tf_op jit(solution)/shard_map/ppermute | solution.py:276
  3.3 17.1 %collective-permute-start.6 = (bf16[2,2,128,128]{3,2,1,0:T(8,128)(2,1)S(1)}, bf16[2,2,128,128]{3,2,1,0:T(8,128)(2,1)S(1)}, u32[]{:S(2)}, u32[]{:S(2)}) collective-permute-start(bf16[2,2,128,128]{3,2,1,0:T(8,128)(2,1)S(1)} %get-tuple-element.36), channel_id=1, source_target_pairs={{0,1},{1,2},{2,3},{3,4},{4,5},{5,6},{6,7},{7,8},{8,9},{9,10},{10,1... | collective-permute-start | bytes 393224 | tf_op jit(solution)/shard_map/ppermute | solution.py:275
  6.0 15.1 %collective-permute-start.7 = (bf16[2,2,128,128]{3,2,1,0:T(8,128)(2,1)S(1)}, bf16[2,2,128,128]{3,2,1,0:T(8,128)(2,1)S(1)}, u32[]{:S(2)}, u32[]{:S(2)}) collective-permute-start(bf16[2,2,128,128]{3,2,1,0:T(8,128)(2,1)S(1)} %get-tuple-element.37), channel_id=1, source_target_pairs={{1,0},{2,1},{3,2},{4,3},{5,4},{6,5},{7,6},{8,7},{9,8},{10,9},{11,1... | collective-permute-start | bytes 393224 | tf_op jit(solution)/shard_map/ppermute | solution.py:276
  11.3 12.3 %collective-permute-start = (bf16[2,2,128,128]{3,2,1,0:T(8,128)(2,1)S(1)}, bf16[2,2,128,128]{3,2,1,0:T(8,128)(2,1)S(1)}, u32[]{:S(2)}, u32[]{:S(2)}) collective-permute-start(bf16[2,2,128,128]{3,2,1,0:T(8,128)(2,1)S(1)} %get-tuple-element.34), channel_id=1, source_target_pairs={{0,1},{1,2},{2,3},{3,4},{4,5},{5,6},{6,7},{7,8},{8,9},{9,10},{10,1... | collective-permute-start | bytes 393224 | tf_op jit(solution)/shard_map/ppermute | solution.py:275
  13.7 11.0 %collective-permute-start.2 = (bf16[2,2,128,128]{3,2,1,0:T(8,128)(2,1)S(1)}, bf16[2,2,128,128]{3,2,1,0:T(8,128)(2,1)S(1)}, u32[]{:S(2)}, u32[]{:S(2)}) collective-permute-start(bf16[2,2,128,128]{3,2,1,0:T(8,128)(2,1)S(1)} %get-tuple-element.34), channel_id=1, source_target_pairs={{496,497},{497,498},{498,499},{499,500},{500,501},{501,502},{502,5... | collective-permute-start | bytes 393224 | tf_op jit(solution)/shard_map/ppermute | solution.py:275
  14.4 10.3 %collective-permute-start.1 = (bf16[2,2,128,128]{3,2,1,0:T(8,128)(2,1)S(1)}, bf16[2,2,128,128]{3,2,1,0:T(8,128)(2,1)S(1)}, u32[]{:S(2)}, u32[]{:S(2)}) collective-permute-start(bf16[2,2,128,128]{3,2,1,0:T(8,128)(2,1)S(1)} %get-tuple-element.35), channel_id=1, source_target_pairs={{1,0},{2,1},{3,2},{4,3},{5,4},{6,5},{7,6},{8,7},{9,8},{10,9},{11,1... | collective-permute-start | bytes 393224 | tf_op jit(solution)/shard_map/ppermute | solution.py:276
  20.5 4.3 %collective-permute-start.3 = (bf16[2,2,128,128]{3,2,1,0:T(8,128)(2,1)S(1)}, bf16[2,2,128,128]{3,2,1,0:T(8,128)(2,1)S(1)}, u32[]{:S(2)}, u32[]{:S(2)}) collective-permute-start(bf16[2,2,128,128]{3,2,1,0:T(8,128)(2,1)S(1)} %get-tuple-element.35), channel_id=1, source_target_pairs={{497,496},{498,497},{499,498},{500,499},{501,500},{502,501},{503,5... | collective-permute-start | bytes 393224 | tf_op jit(solution)/shard_map/ppermute | solution.py:276
  21.6 21.5 %collective-permute-start.8 = (bf16[2,2,128,128]{3,2,1,0:T(8,128)(2,1)S(1)}, bf16[2,2,128,128]{3,2,1,0:T(8,128)(2,1)S(1)}, u32[]{:S(2)}, u32[]{:S(2)}) collective-permute-start(bf16[2,2,128,128]{3,2,1,0:T(8,128)(2,1)S(1)} %get-tuple-element.38), channel_id=1, source_target_pairs={{0,16},{16,32},{32,48},{48,64},{64,80},{80,96},{96,112},{112,128},... | collective-permute-start | bytes 393224 | tf_op jit(solution)/shard_map/ppermute | solution.py:280
